TPU v7x, 256 devices: a whole 4x4x8 slice. The times are simulated.
256 devices in a mesh: zone: 8 (over x, z_lo), dom: 32 (over y, z_hi, core).
Axes of the slice: x: 4, y: 4, z: 8 (z_hi: 4, z_lo: 2; z = z_hi * 2 + z_lo), core: 2. Of those that a mesh axis runs over, the one named last changes fastest.
Arguments:
- state: float32 [8, 32, 5, 512], P('zone', 'dom'), as said below
- grad_op: bfloat16 [8, 32, 4, 3, 128, 384], P('zone', 'dom'), may hold values from -0.3125 to 0.3125
- adjacency: int32 [8, 32, 4, 3], P('zone', 'dom'), may hold values from 0 to 3, as said below
- node_vel: float32 [8, 32, 3, 512], P('zone', 'dom'), may hold values from -5 to 5
- face_normal: float32 [8, 32, 3, 25600], P('zone', 'dom'), as said below
- face_nodes: int32 [8, 32, 4, 25600], P('zone', 'dom'), may hold values from 0 to 767
- inner_cells: int32 [8, 32, 2, 1024], P('zone', 'dom'), may hold values from 0 to 511
- iface_cells: int32 [8, 32, 6, 4096], P('zone', 'dom'), may hold values from 0 to 511
- cell_volume: float32 [8, 32, 512], P('zone', 'dom'), may hold values from 0.5 to 2
- block_counts: int32 [8, 32], P('zone', 'dom'), may hold values from 1 to 4, as said below
Outputs:
- content: float32 [8, 32, 5, 512], P('zone', 'dom')
- new_volume: float32 [8, 32, 512], P('zone', 'dom')
Inputs may be any that keep to these rules, and one draw needn't show every extreme that they name: `state`: density 0.5 to 2, velocity components -0.3 to 0.3 and pressure 1 to 2 in every cell, stored as conserved variables. `adjacency`: entry 0 of each block's stencil is the block itself. `face_normal`: every area vector has length 0.5 to 1.5. `block_counts`: at least one partition has all 4 blocks live.
All inputs are finite; a program needn't handle non-finite values.
Results may differ from a plain program's by a relative error of at most 0.00054.
Values sent between devices are 32-bit elements; how exact they have to be, the bound alone decides.
A program may use at most 128 MiB of HBM per device.

v0:
```python
import jax
import jax.numpy as jnp
from jax import lax
from jax.sharding import PartitionSpec as P

CB = 128
ROUNDS = 6
HN = 128


GAMMA_LESS = 0.4
STEP_SIZE = 0.25
RECON_GAIN = 0.2
FIX_SHARE = 0.1


def with_halo(cells, sides, width):
    for axis, dim in sides:
        count = lax.axis_size(axis)
        ends = count - 1
        head = lax.slice_in_dim(cells, 0, width, axis=dim)
        tail = lax.slice_in_dim(cells, cells.shape[dim] - width, cells.shape[dim], axis=dim)
        cells = jnp.concatenate(
            [
                lax.ppermute(tail, axis, [(i, (i + 1) % count) for i in range(ends)]),
                cells,
                lax.ppermute(head, axis, [((i + 1) % count, i) for i in range(ends)]),
            ],
            axis=dim,
        )
    return cells


def partner(shard, axis, apart):
    return lax.ppermute(shard, axis, [(i, i ^ 1 << apart) for i in range(lax.axis_size(axis))])


def primitives(face_states):
    density = face_states[0]
    velocity = face_states[1:4] / density
    pressure = GAMMA_LESS * (face_states[4] - 0.5 * density * jnp.sum(velocity * velocity, axis=0))
    enthalpy = (face_states[4] + pressure) / density
    return (density, velocity, pressure, enthalpy)


def rebuild(values, slopes, normal):
    delta = jnp.sum(slopes * normal[None], axis=1)
    density = values[0]
    energy = values[4]
    new_density = density * (1.0 + RECON_GAIN * jnp.tanh(delta[0] / density))
    new_momentum = values[1:4] + RECON_GAIN * density * jnp.tanh(delta[1:4] / density)
    new_energy = energy * (1.0 + RECON_GAIN * jnp.tanh(delta[4] / energy))
    return jnp.concatenate([new_density[None], new_momentum, new_energy[None]], axis=0)


def physical(face_states, velocity, pressure, unit_normal, grid_speed):
    normal_speed = jnp.sum(velocity * unit_normal, axis=0)
    moving = normal_speed - grid_speed
    mass_flux = face_states[0] * moving
    momentum = face_states[1:4] * moving + pressure * unit_normal
    energy = face_states[4] * moving + pressure * normal_speed
    return jnp.concatenate([mass_flux[None], momentum, energy[None]], axis=0)


def roe_flux(left_side, right_side, normal, sweeps):
    face_area = jnp.sqrt(jnp.sum(normal * normal, axis=0))
    unit_normal = normal / face_area
    grid_speed = sweeps / (STEP_SIZE * face_area)
    dens_left, vel_left, pres_left, enth_left = primitives(left_side)
    dens_right, vel_right, pres_right, enth_right = primitives(right_side)
    root_left = jnp.sqrt(dens_left)
    root_right = jnp.sqrt(dens_right)
    weight_sum = root_left + root_right
    mean_vel = (root_left * vel_left + root_right * vel_right) / weight_sum
    mean_enth = (root_left * enth_left + root_right * enth_right) / weight_sum
    mean_dens = root_left * root_right
    mean_normal = jnp.sum(mean_vel * unit_normal, axis=0)
    kinetic = 0.5 * jnp.sum(mean_vel * mean_vel, axis=0)
    sound_speed = jnp.sqrt(GAMMA_LESS * (mean_enth - kinetic))
    sound_sq = sound_speed * sound_speed
    jump_pres = pres_right - pres_left
    jump_dens = dens_right - dens_left
    jump_vel = vel_right - vel_left
    jump_normal = jnp.sum(jump_vel * unit_normal, axis=0)
    entropy_fix = (FIX_SHARE * sound_speed) ** 2
    wave_slow = jnp.sqrt((mean_normal - sound_speed - grid_speed) ** 2 + entropy_fix)
    wave_mid = jnp.sqrt((mean_normal - grid_speed) ** 2 + entropy_fix)
    wave_fast = jnp.sqrt((mean_normal + sound_speed - grid_speed) ** 2 + entropy_fix)
    amp_slow = (jump_pres - mean_dens * sound_speed * jump_normal) / (2.0 * sound_sq)
    amp_fast = (jump_pres + mean_dens * sound_speed * jump_normal) / (2.0 * sound_sq)
    amp_mid = jump_dens - jump_pres / sound_sq
    shear = jump_vel - jump_normal * unit_normal
    slow_part = wave_slow * amp_slow
    fast_part = wave_fast * amp_fast
    diss_mass = slow_part + wave_mid * amp_mid + fast_part
    diss_mom = (
        slow_part * (mean_vel - sound_speed * unit_normal)
        + wave_mid * (amp_mid * mean_vel + mean_dens * shear)
        + fast_part * (mean_vel + sound_speed * unit_normal)
    )
    diss_energy = (
        slow_part * (mean_enth - sound_speed * mean_normal)
        + wave_mid
        * (
            amp_mid * kinetic
            + mean_dens * (jnp.sum(mean_vel * jump_vel, axis=0) - mean_normal * jump_normal)
        )
        + fast_part * (mean_enth + sound_speed * mean_normal)
    )
    dissipation = jnp.concatenate([diss_mass[None], diss_mom, diss_energy[None]], axis=0)
    central = physical(left_side, vel_left, pres_left, unit_normal, grid_speed) + physical(
        right_side, vel_right, pres_right, unit_normal, grid_speed
    )
    return face_area * 0.5 * (central - dissipation)


def cell_slopes(values, grad_blocks, neighbours):
    nblocks = neighbours.shape[0]
    blocks = values.astype(jnp.bfloat16).reshape(5, nblocks, CB)
    nearby = blocks[:, neighbours]
    products = jnp.einsum("vbkj,bkjc->vbc", nearby, grad_blocks, preferred_element_type=jnp.float32)
    return products.reshape(5, nblocks, 3, CB).transpose(0, 2, 1, 3).reshape(5, 3, nblocks * CB)


def shards(
    state,
    grad_op,
    adjacency,
    node_vel,
    face_normal,
    face_nodes,
    inner_cells,
    iface_cells,
    cell_volume,
    block_counts,
):
    values = state[0, 0]
    normal = face_normal[0, 0]
    cell_count = values.shape[1]
    face_count = normal.shape[1]
    extended = with_halo(node_vel[0, 0], (("dom", 1),), HN)
    slopes = cell_slopes(values, grad_op[0, 0], adjacency[0, 0])
    node_lists = face_nodes[0, 0]
    node_picked = jnp.take(extended, node_lists.reshape(-1), axis=1).reshape(3, 4, face_count)
    mean_vel = 0.25 * (
        node_picked[:, 0] + node_picked[:, 1] + node_picked[:, 2] + node_picked[:, 3]
    )
    sweeps = STEP_SIZE * jnp.sum(normal * mean_vel, axis=0)
    cell_pairs = inner_cells[0, 0]
    face_cells = iface_cells[0, 0]
    count_inner = cell_pairs.shape[1]
    round_count = face_cells.shape[0]
    slot_count = face_cells.shape[1]
    all_cells = jnp.concatenate([cell_pairs[0], cell_pairs[1], face_cells.reshape(-1)], axis=0)
    cell_table = jnp.concatenate([values, slopes.reshape(15, cell_count)], axis=0)
    picked = jnp.take(cell_table, all_cells, axis=1)
    left_cols = picked[:, :count_inner]
    right_cols = picked[:, count_inner : 2 * count_inner]
    iface_cols = picked[:, 2 * count_inner :].reshape(20, round_count, slot_count)
    inner_normal = normal[:, :count_inner]
    inner_sweeps = sweeps[:count_inner]
    left_side = rebuild(left_cols[:5], left_cols[5:].reshape(5, 3, count_inner), inner_normal)
    right_side = rebuild(right_cols[:5], right_cols[5:].reshape(5, 3, count_inner), -inner_normal)
    inner_flux = roe_flux(left_side, right_side, inner_normal, inner_sweeps)
    iface_normal = normal[:, count_inner:].reshape(3, round_count, slot_count)
    iface_sweeps = sweeps[count_inner:].reshape(round_count, slot_count)
    own_faces = rebuild(
        iface_cols[:5], iface_cols[5:].reshape(5, 3, round_count, slot_count), iface_normal
    )
    payloads = []
    for round_index in range(ROUNDS):
        payloads.append(own_faces[:, round_index])
    received = []
    for bit_number in range(4):
        received.append(partner(payloads[bit_number], "dom", bit_number))
    received.append(partner(payloads[4], "zone", 0))
    received.append(partner(payloads[5], ("zone", "dom"), 4))
    outer_list = []
    for incoming in received:
        outer_list.append(incoming)
    theirs = jnp.stack(outer_list, axis=1)
    iface_flux = roe_flux(own_faces, theirs, iface_normal, iface_sweeps).reshape(
        5, round_count * slot_count
    )
    flux_terms = jnp.concatenate([-inner_flux, inner_flux, -iface_flux], axis=1)
    sweep_terms = jnp.concatenate([inner_sweeps, -inner_sweeps, iface_sweeps.reshape(-1)], axis=0)
    terms = jnp.concatenate([flux_terms, sweep_terms[None]], axis=0)
    totals = jnp.zeros((6, cell_count), jnp.float32).at[:, all_cells].add(terms)
    residual = totals[:5]
    change = totals[5]
    volume = cell_volume[0, 0]
    live_cells = jnp.arange(cell_count) // CB < block_counts[0, 0]
    content = volume[None] * values + jnp.where(live_cells[None], STEP_SIZE * residual, 0.0)
    new_volume = volume + jnp.where(live_cells, change, 0.0)
    return (content[None, None], new_volume[None, None])


def solution(mesh):
    return jax.shard_map(
        shards,
        mesh=mesh,
        in_specs=(
            P("zone", "dom", None, None),
            P("zone", "dom", None, None, None, None),
            P("zone", "dom", None, None),
            P("zone", "dom", None, None),
            P("zone", "dom", None, None),
            P("zone", "dom", None, None),
            P("zone", "dom", None, None),
            P("zone", "dom", None, None),
            P("zone", "dom", None),
            P("zone", "dom"),
        ),
        out_specs=(P("zone", "dom", None, None), P("zone", "dom", None)),
        check_vma=False,
    )
```

profile of v0, /device:TPU:199, one launch (start us, length us, event | category | flops | bytes accessed | tf_op | source)
XLA Modules:
  0.0 677.6 jit_solution(14768179975790822995)
XLA Ops:
  0.6 0.8 copy.357
  1.4 0.6 fusion.105
  2.0 2.6 collective-permute-start.1
  4.6 6.0 collective-permute-start
  10.6 0.7 convert_reduce_fusion
  11.3 0.8 copy.243
  12.2 0.8 fusion.104
  13.0 0.7 compare_select_fusion.4
  13.9 0.6 gather_fusion
  14.5 0.3 fusion.2
  14.9 1.0 compare_select_fusion.2
  16.0 0.6 copy-done.11
  16.7 88.1 %gather_fusion.1 = f32[26624,20]{1,0:T(8,128)} fusion(f32[20,512]{0,1:T(8,128)S(1)} %pad_maximum_fusion, s32[26624]{0:T(1024)S(1)} %broadcast_clamp_fusion.1), kind=kCustom, calls=%fused_computation.1 | custom fusion | bytes 4366336 | tf_op jit(solution)/shard_map/jit(_take)/gather | solution.py:156
  104.8 9.3 %copy.248 = f32[26624,20]{0,1:T(8,128)} copy(f32[26624,20]{1,0:T(8,128)} %gather_fusion.1) | data formatting | bytes 4259840 | tf_op jit(solution)/shard_map/jit(_take)/gather | solution.py:156
  114.1 1.9 select_bitcast_fusion
  116.1 2.0 slice_reduce_fusion.2
  118.1 1.3 slice.241
  119.6 0.9 fusion.103
  120.5 0.7 squeeze.100
  121.2 2.2 reshape.563
  123.4 1.0 mul.1165
  124.4 0.7 squeeze.102
  125.3 1.3 multiply_reduce_fusion
  126.7 1.7 sqrt_bitcast_fusion
  128.5 0.5 pad_maximum_fusion.2
  128.9 0.7 copy.355
  129.6 0.7 copy.354
  130.4 0.7 copy.353
  131.1 0.3 collective-permute-start.4
  131.3 0.4 copy.278
  131.8 0.2 compare_and_fusion
  132.0 1.0 fusion.101
  133.0 0.7 multiply_reduce_fusion.20
  133.7 0.4 compare_select_fusion
  135.1 1.5 sqrt_multiply_fusion.1
  136.6 1.4 multiply_reduce_fusion.16
  138.1 2.0 multiply_reduce_fusion.18
  140.1 0.5 fusion.74
  140.6 0.7 copy.352
  141.3 0.7 copy.351
  142.0 0.7 copy.356
  142.7 2.2 collective-permute-start.5
  144.9 0.7 collective-permute-start.6
  145.7 0.7 pad_maximum_fusion.9
  146.5 336.4 %gather_fusion.2 = f32[102400,3]{1,0:T(8,128)} fusion(f32[3,768]{0,1:T(8,128)S(1)} %copy.249, s32[102400]{0:T(1024)S(1)} %broadcast_clamp_fusion), kind=kCustom, calls=%fused_computation.2 | custom fusion | bytes 2867200 | tf_op jit(solution)/shard_map/jit(_take)/gather | solution.py:144
  482.9 27.2 %copy.251 = f32[3,4,25600]{2,0,1:T(4,128)S(1)} copy(f32[3,4,25600]{0,2,1:T(8,128)} %bitcast.282) | data formatting | bytes 2457600 | tf_op jit(solution)/shard_map/jit(_take)/gather | solution.py:144
  510.3 0.6 broadcast_select_fusion
  511.0 0.5 fusion.11
  512.3 3.0 collective-permute-start.7
  515.3 0.9 bitcast_dynamic-update-slice_fusion.5
  516.2 0.9 bitcast_dynamic-update-slice_fusion.4
  517.1 0.9 bitcast_dynamic-update-slice_fusion.3
  518.1 0.9 bitcast_dynamic-update-slice_fusion.2
  519.0 0.9 bitcast_dynamic-update-slice_fusion.1
  520.2 2.6 multiply_reduce_fusion.4
  522.8 0.5 add_bitcast_fusion
  523.3 0.3 fusion.82
  524.3 0.9 multiply_add_fusion
  525.2 0.8 fusion.7
  526.3 7.8 %copy.262 = f32[26624,6]{1,0:T(8,128)} copy(f32[26624,6]{0,1:T(8,128)S(1)} %maximum_bitcast_fusion) | data formatting | bytes 1277952 | tf_op jit(solution)/shard_map/concatenate | solution.py:187
  534.1 141.8 %scatter_custom_fusion = f32[6,512]{0,1:T(8,128)S(1)} fusion(s32[26624]{0:T(1024)} %bitcast.303, f32[26624,6]{1,0:T(8,128)} %copy.262, f32[]{:T(128)} %constant.29.clone.1), kind=kCustom, calls=%fused_computation.141 | custom fusion | flops 159744 | bytes 12800 | tf_op jit(solution)/shard_map/scatter-add | solution.py:188
  675.8 0.2 slice_reduce_fusion
  676.3 0.7 copy.263
  677.0 0.6 fusion.77
  (145 shorter events, 3.6 us)
Async XLA Ops:
  0.6 13.8 %copy-start = (bf16[1,1,4,3,128,384]{5,4,3,2,1,0:T(8,128)(2,1)S(1)}, bf16[1,1,4,3,128,384]{5,4,3,2,1,0:T(8,128)(2,1)}, u32[]{:S(2)}) copy-start(bf16[1,1,4,3,128,384]{5,4,3,2,1,0:T(8,128)(2,1)} %param.11) | copy-start | bytes 3538948
  1.4 9.2 %copy-start.20 = (f32[1,1,3,512]{3,2,1,0:T(4,128)}, f32[1,1,3,512]{3,2,1,0:T(4,128)S(1)}, u32[]{:S(2)}) copy-start(f32[1,1,3,512]{3,2,1,0:T(4,128)S(1)} %copy.357) | copy-start | bytes 18436
  2.0 140.7 %collective-permute-start.1 = (f32[3,128]{1,0:T(4,128)}, f32[3,128]{1,0:T(4,128)}, u32[]{:S(2)}, u32[]{:S(2)}) collective-permute-start(f32[3,128]{1,0:T(4,128)} %get-tuple-element.136), channel_id=1, source_target_pairs={{1,0},{2,1},{3,2},{4,3},{5,4},{6,5},{7,6},{8,7},{9,8},{10,9},{11,1... | collective-permute-start | bytes 4616 | tf_op jit(solution)/shard_map/ppermute | solution.py:27
  4.6 140.3 %collective-permute-start = (f32[3,128]{1,0:T(4,128)}, f32[3,128]{1,0:T(4,128)}, u32[]{:S(2)}, u32[]{:S(2)}) collective-permute-start(f32[3,128]{1,0:T(4,128)} %get-tuple-element.135), channel_id=1, source_target_pairs={{0,1},{1,2},{2,3},{3,4},{4,5},{5,6},{6,7},{7,8},{8,9},{9,10},{10,1... | collective-permute-start | bytes 4616 | tf_op jit(solution)/shard_map/ppermute | solution.py:25
  12.2 92.6 %copy-start.3 = (f32[1,1,5,512]{2,3,1,0:T(8,128)}, f32[1,1,5,512]{2,3,1,0:T(8,128)S(1)}, u32[]{:S(2)}) copy-start(f32[1,1,5,512]{2,3,1,0:T(8,128)S(1)} %copy.243) | copy-start | bytes 30724
  15.9 0.6 copy-start.11
  104.8 9.3 %copy-start.13 = (s32[1,1,6,4096]{3,1,2,0:T(1,128)S(1)}, s32[1,1,6,4096]{3,1,2,0:T(1,128)}, u32[]{:S(2)}) copy-start(s32[1,1,6,4096]{3,1,2,0:T(1,128)} %param.17) | copy-start | bytes 294916
  116.1 3.5 copy-start.2
  116.1 3.4 copy-start.7
  119.6 4.8 copy-start.5
  119.6 4.8 copy-start.15
  121.2 4.1 copy-start.14
  125.3 1.4 copy-start.10
  126.6 4.7 copy-start.6
  129.6 382.6 %collective-permute-start.2 = (f32[5,4096]{1,0:T(8,128)}, f32[5,4096]{1,0:T(8,128)}, u32[]{:S(2)}, u32[]{:S(2)}) collective-permute-start(f32[5,4096]{1,0:T(8,128)} %bitcast.277), channel_id=1, source_target_pairs={{0,1},{1,0},{2,3},{3,2},{4,5},{5,4},{6,7},{7,6},{8,9},{9,8},{10,11... | collective-permute-start | bytes 245768 | tf_op jit(solution)/shard_map/ppermute | solution.py:35
  130.4 385.8 %collective-permute-start.3 = (f32[5,4096]{1,0:T(8,128)}, f32[5,4096]{1,0:T(8,128)}, u32[]{:S(2)}, u32[]{:S(2)}) collective-permute-start(f32[5,4096]{1,0:T(8,128)} %bitcast.276), channel_id=1, source_target_pairs={{0,2},{1,3},{2,0},{3,1},{4,6},{5,7},{6,4},{7,5},{8,10},{9,11},{10,... | collective-permute-start | bytes 245768 | tf_op jit(solution)/shard_map/ppermute | solution.py:35
  130.4 15.3 %copy-start.21 = (f32[1,1,3,512]{3,2,1,0:T(4,128)S(1)}, f32[1,1,3,512]{3,2,1,0:T(4,128)}, u32[]{:S(2)}) copy-start(f32[1,1,3,512]{3,2,1,0:T(4,128)} %copy-done.20) | copy-start | bytes 18436
  131.1 386.1 %collective-permute-start.4 = (f32[5,4096]{1,0:T(8,128)}, f32[5,4096]{1,0:T(8,128)}, u32[]{:S(2)}, u32[]{:S(2)}) collective-permute-start(f32[5,4096]{1,0:T(8,128)} %bitcast.275), channel_id=1, source_target_pairs={{0,4},{1,5},{2,6},{3,7},{4,0},{5,1},{6,2},{7,3},{8,12},{9,13},{10,... | collective-permute-start | bytes 245768 | tf_op jit(solution)/shard_map/ppermute | solution.py:35
  133.7 2.9 copy-start.26
  136.6 1.5 copy-start.29
  136.6 9.1 %copy-start.31 = (f32[1,1024]{1,0:T(1,128)}, f32[1,1024]{1,0:T(1,128)S(1)}, u32[]{:S(2)}) copy-start(f32[1,1024]{1,0:T(1,128)S(1)} %get-tuple-element.82) | copy-start | bytes 12292
  142.7 375.3 %collective-permute-start.5 = (f32[5,4096]{1,0:T(8,128)}, f32[5,4096]{1,0:T(8,128)}, u32[]{:S(2)}, u32[]{:S(2)}) collective-permute-start(f32[5,4096]{1,0:T(8,128)} %bitcast.274), channel_id=1, source_target_pairs={{0,8},{1,9},{2,10},{3,11},{4,12},{5,13},{6,14},{7,15},{8,0},{9,1},... | collective-permute-start | bytes 245768 | tf_op jit(solution)/shard_map/ppermute | solution.py:35
  144.9 374.0 %collective-permute-start.6 = (f32[5,4096]{1,0:T(8,128)}, f32[5,4096]{1,0:T(8,128)}, u32[]{:S(2)}, u32[]{:S(2)}) collective-permute-start(f32[5,4096]{1,0:T(8,128)} %bitcast.273), channel_id=1, source_target_pairs={{0,32},{32,0},{64,96},{96,64},{128,160},{160,128},{192,224},{224,1... | collective-permute-start | bytes 245768 | tf_op jit(solution)/shard_map/ppermute | solution.py:35
  510.1 1.0 copy-start.8
  510.1 1.5 copy-start.12
  510.1 1.6 copy-start.19
  510.1 1.6 copy-start.22
  510.1 1.6 copy-start.23
  510.1 1.6 copy-start.24
  510.1 1.6 copy-start.25
  510.1 1.6 copy-start.27
  510.1 1.6 copy-start.30
  510.2 1.6 copy-start.32
  510.2 1.6 copy-start.34
  510.2 1.6 copy-start.35
  510.2 1.6 copy-start.37
  510.2 1.6 copy-start.38
  510.2 1.6 copy-start.33
  510.2 1.6 copy-start.28
  510.2 1.6 copy-start.41
  510.2 1.7 copy-start.39
  510.2 1.7 copy-start.40
  511.0 1.0 copy-start.17
  511.0 1.0 copy-start.18
  511.0 1.0 copy-start.36
  511.0 1.2 copy-start.16
  511.5 8.7 %copy-start.9 = (f32[6,4096]{1,0:T(8,128)S(1)}, f32[6,4096]{1,0:T(8,128)}, u32[]{:S(2)}) copy-start(f32[6,4096]{1,0:T(8,128)} %get-tuple-element.73) | copy-start | bytes 294916
  512.3 7.6 %collective-permute-start.7 = (f32[5,4096]{1,0:T(8,128)S(1)}, f32[5,4096]{1,0:T(8,128)S(1)}, u32[]{:S(2)}, u32[]{:S(2)}) collective-permute-start(f32[5,4096]{1,0:T(8,128)S(1)} %bitcast.315), channel_id=1, source_target_pairs={{0,16},{1,17},{2,18},{3,19},{4,20},{5,21},{6,22},{7,23},{8,24},{9,... | collective-permute-start | bytes 245768 | tf_op jit(solution)/shard_map/ppermute | solution.py:35
  526.2 149.9 %copy-start.4 = (f32[1,1,5,512]{2,3,1,0:T(8,128)S(1)}, f32[1,1,5,512]{2,3,1,0:T(8,128)}, u32[]{:S(2)}) copy-start(f32[1,1,5,512]{2,3,1,0:T(8,128)} %copy-done.3) | copy-start | bytes 30724
  526.2 149.9 %copy-start.42 = (f32[1,1,512]{2,1,0:T(1,128)S(1)}, f32[1,1,512]{2,1,0:T(1,128)}, u32[]{:S(2)}) copy-start(f32[1,1,512]{2,1,0:T(1,128)} %param.18) | copy-start | bytes 6148
  526.2 149.9 %copy-start.43 = (pred[512]{0:T(512)(128)(4,1)S(1)}, pred[512]{0:T(512)(128)(4,1)}, u32[]{:S(2)}) copy-start(pred[512]{0:T(512)(128)(4,1)} %fusion.74) | copy-start | bytes 1540
  526.2 151.4 %copy-start.1 = (bf16[1,1,4,3,128,384]{5,4,3,2,1,0:T(8,128)(2,1)S(1)}, bf16[1,1,4,3,128,384]{5,4,3,2,1,0:T(8,128)(2,1)}, u32[]{:S(2)}) copy-start(bf16[1,1,4,3,128,384]{5,4,3,2,1,0:T(8,128)(2,1)} %param.11) | copy-start | bytes 3538948
where the time goes:
time: 686 us; the launch traced here: 678 us
  local copies, waits for them, and re-layouts  494 us (72%)
  other arithmetic  166 us (24%)
  starting transfers between devices  14.8 us (2%)
    gather x2, local copies, waits for them, and re-layouts, shards(): jnp.take(extended, node_lists.reshape(-1), axis=1).reshape(3, 4, face_count)  364 us
    scatter-add x1, other arithmetic, shards(): totals = jnp.zeros((6, cell_count), jnp.float32).at[:, all_cells].add(terms)  142 us
    gather x2, local copies, waits for them, and re-layouts, shards(): picked = jnp.take(cell_table, all_cells, axis=1)  97.3 us
  transfers between devices with their start and end apart: 8, of which 0 were waited for; matrix products, arithmetic and copies ran while one was open for 74% of the time, Pallas kernels for 0%

commit v1 on v0

v1 whole, which is shorter than its diff:
```python
import functools

import jax
import jax.numpy as jnp
from jax import lax
from jax.experimental import pallas as pl
from jax.experimental.pallas import tpu as pltpu
from jax.sharding import PartitionSpec as P

CB = 128
NB = 4
K = 3
ROUNDS = 6
HN = 128
NN = 512
RT = 4
TILES = 25
RS = 56

STEP_SIZE = 0.25
RECON_GAIN = 0.2
GAMMA_LESS = 0.4

SEND_ORDER = (2, 1, 5, 4, 3, 0)
FLUX_ORDER = (2, 1, 5, 4, 3, 0)

F32 = jnp.float32
BF16 = jnp.bfloat16


def take(row, lanes):
    return jnp.take_along_axis(row, lanes, axis=1, mode="promise_in_bounds")


def rows8(tile):
    return pl.ds(pl.multiple_of(tile * 8, 8), 8)


def split_cells(cells):
    return cells & 127, (cells & 128) != 0, (cells & 256) != 0


def pick(table, first, where):
    lanes, odd, upper = where
    low = jnp.where(odd, take(table[first + 1], lanes), take(table[first], lanes))
    high = jnp.where(odd, take(table[first + 3], lanes), take(table[first + 2], lanes))
    return jnp.where(upper, high, low)


def rebuild(table, where, normal):
    cons = [pick(table, 4 * v, where) for v in range(5)]
    delta = []
    for v in range(5):
        parts = [pick(table, 20 + 4 * (3 * v + d), where) * normal[d] for d in range(3)]
        delta.append(parts[0] + parts[1] + parts[2])
    per_dens = 1.0 / cons[0]
    gain = RECON_GAIN * cons[0]
    out = [cons[0] + gain * jnp.tanh(delta[0] * per_dens)]
    for v in range(1, 4):
        out.append(cons[v] + gain * jnp.tanh(delta[v] * per_dens))
    out.append(cons[4] + RECON_GAIN * cons[4] * jnp.tanh(delta[4] / cons[4]))
    return out


def dot3(a, b):
    return a[0] * b[0] + a[1] * b[1] + a[2] * b[2]


def side_values(cons, unit):
    per_dens = 1.0 / cons[0]
    vel = [cons[i] * per_dens for i in (1, 2, 3)]
    pres = GAMMA_LESS * (cons[4] - 0.5 * dot3(cons[1:4], vel))
    enth = (cons[4] + pres) * per_dens
    return vel, pres, enth, dot3(vel, unit)


def roe_flux(left, right, normal, sweep):
    area_sq = dot3(normal, normal)
    per_area = lax.rsqrt(area_sq)
    area = area_sq * per_area
    unit = [x * per_area for x in normal]
    grid = sweep * per_area * (1.0 / STEP_SIZE)
    vel_l, pres_l, enth_l, q_l = side_values(left, unit)
    vel_r, pres_r, enth_r, q_r = side_values(right, unit)
    root_l = jnp.sqrt(left[0])
    root_r = jnp.sqrt(right[0])
    per_sum = 1.0 / (root_l + root_r)
    a = root_l * per_sum
    b = root_r * per_sum
    vel = [a * x + b * y for x, y in zip(vel_l, vel_r)]
    enth = a * enth_l + b * enth_r
    dens = root_l * root_r
    q = dot3(vel, unit)
    kinetic = 0.5 * dot3(vel, vel)
    c_sq = GAMMA_LESS * (enth - kinetic)
    c = jnp.sqrt(c_sq)
    per_c_sq = 1.0 / c_sq
    d_pres = pres_r - pres_l
    d_dens = right[0] - left[0]
    d_vel = [y - x for x, y in zip(vel_l, vel_r)]
    d_q = dot3(d_vel, unit)
    fix = 0.01 * c_sq
    rel = q - grid
    slow = rel - c
    fast = rel + c
    wave_slow = jnp.sqrt(slow * slow + fix)
    wave_mid = jnp.sqrt(rel * rel + fix)
    wave_fast = jnp.sqrt(fast * fast + fix)
    half = 0.5 * per_c_sq
    cross = dens * c * d_q
    part_slow = wave_slow * ((d_pres - cross) * half)
    part_fast = wave_fast * ((d_pres + cross) * half)
    part_mid = wave_mid * (d_dens - d_pres * per_c_sq)
    shear = wave_mid * dens
    both = part_slow + part_fast
    total = both + part_mid
    diff = c * (part_fast - part_slow)
    move_l = q_l - grid
    move_r = q_r - grid
    along = pres_l + pres_r - diff + shear * d_q
    out = [left[0] * move_l + right[0] * move_r - total]
    for i in range(3):
        out.append(
            left[i + 1] * move_l
            + right[i + 1] * move_r
            + along * unit[i]
            - total * vel[i]
            - shear * d_vel[i]
        )
    out.append(
        left[4] * move_l
        + right[4] * move_r
        + pres_l * q_l
        + pres_r * q_r
        - both * enth
        - diff * q
        - part_mid * kinetic
        - shear * (dot3(vel, d_vel) - q * d_q)
    )
    scale = 0.5 * area
    return [scale * x for x in out]


def scatter(terms, where_cells, masked, total):
    lanes = where_cells & 127
    chunk = where_cells >> 7
    for v, x in enumerate(terms):
        upper = x.astype(BF16).astype(F32)
        for piece, part in enumerate((upper, x - upper)):
            for h in range(4):
                masked[pl.ds(h * 12 + piece * 6 + v, 8, stride=RS), :] = jnp.where(chunk == h, part, 0.0)
    slot = lax.broadcasted_iota(jnp.int32, (128, 128), 0)
    result = None
    for s in range(0, 8, 2):
        pair = (s, s + 1)
        left = jnp.concatenate([masked[i * RS : i * RS + 48, :].astype(BF16) for i in pair], axis=1)
        right = jnp.concatenate(
            [jnp.where(lanes[i : i + 1, :] == slot, 1.0, 0.0).astype(BF16) for i in pair], axis=1
        )
        part = lax.dot_general(left, right, (((1,), (1,)), ((), ())), preferred_element_type=F32)
        result = part if result is None else result + part
    total[...] += result


def kernel(
    remote,
    state,
    grad,
    adjacency,
    node_vel,
    face_normal,
    face_nodes,
    inner_cells,
    iface_cells,
    volume,
    counts,
    content,
    new_volume,
    table,
    nodes,
    normals,
    lists,
    pairs,
    cells,
    own,
    theirs,
    sweeps,
    halo,
    masked,
    total,
    send_sem,
    recv_sem,
    halo_send,
    halo_recv,
):
    if remote:
        zone = lax.axis_index("zone")
        dom = lax.axis_index("dom")
        n_dom = lax.axis_size("dom")
        nxt = lax.rem(dom + 1, n_dom)
        prv = lax.rem(dom + n_dom - 1, n_dom)

        def flip(at, bit):
            return at + bit * (1 - 2 * ((at // bit) % 2))

        peers = [
            (zone, flip(dom, 1)),
            (zone, flip(dom, 2)),
            (zone, flip(dom, 4)),
            (zone, flip(dom, 8)),
            (flip(zone, 1), dom),
            (zone, flip(dom, 16)),
        ]
        barrier = pltpu.get_barrier_semaphore()
        for peer in peers + [(zone, nxt), (zone, prv)]:
            pl.semaphore_signal(barrier, inc=1, device_id=peer, device_id_type=pl.DeviceIdType.MESH)

    def exchange(index):
        if remote:
            return pltpu.make_async_remote_copy(
                src_ref=own.at[index],
                dst_ref=theirs.at[index],
                send_sem=send_sem.at[index],
                recv_sem=recv_sem.at[index],
                device_id=peers[index],
                device_id_type=pl.DeviceIdType.MESH,
            )
        return pltpu.make_async_copy(own.at[index], theirs.at[index], recv_sem.at[index])

    def halo_copy(side):
        source = node_vel.at[:, pl.ds((NN - HN) * (1 - side), HN)]
        if remote:
            return pltpu.make_async_remote_copy(
                src_ref=source,
                dst_ref=halo.at[side],
                send_sem=halo_send.at[side],
                recv_sem=halo_recv.at[side],
                device_id=(zone, prv if side else nxt),
                device_id_type=pl.DeviceIdType.MESH,
            )
        return pltpu.make_async_copy(source, halo.at[side], halo_recv.at[side])

    for v in range(5):
        for h in range(4):
            table[4 * v + h] = jnp.broadcast_to(state[v : v + 1, h * CB : (h + 1) * CB], (8, CB))
    for b in range(NB):
        sums = None
        for k in range(K):
            near = jnp.full((5, CB), adjacency[b, k], jnp.int32)
            block = state[:, 0:CB]
            for other in range(1, NB):
                block = jnp.where(near == other, state[:, other * CB : (other + 1) * CB], block)
            part = jnp.dot(block.astype(BF16), grad[b, k], preferred_element_type=F32)
            sums = part if sums is None else sums + part
        for v in range(5):
            for d in range(3):
                table[20 + 4 * (3 * v + d) + b] = jnp.broadcast_to(
                    sums[v : v + 1, d * CB : (d + 1) * CB], (8, CB)
                )

    def spread(chunk, _):
        at = pl.ds(pl.multiple_of(chunk * CB, CB), CB)
        normals[pl.ds(chunk * 4, 3), :] = face_normal[:, at]
        return 0

    lax.fori_loop(0, TILES * 8, spread, 0, unroll=8)

    def spread_cells(chunk, _):
        at = pl.ds(pl.multiple_of(chunk * CB, CB), CB)
        cells[pl.ds(pl.multiple_of(chunk * 8, 8), ROUNDS), :] = iface_cells[:, at]
        return 0

    lax.fori_loop(0, RT * 8, spread_cells, 0, unroll=8)

    def normal_of(tile):
        return [normals[pl.ds(tile * 32 + d, 8, stride=4), :] for d in range(3)]

    def cells_of(index, t):
        return cells[pl.ds(t * 64 + index, 8, stride=8), :]

    if remote:
        pl.semaphore_wait(barrier, len(peers) + 2)
    for side in range(2):
        halo_copy(side).start()

    for index in SEND_ORDER:

        def own_tile(t, _, index=index):
            where = split_cells(cells_of(index, t))
            out = rebuild(table, where, normal_of(1 + RT * index + t))
            for v in range(5):
                own[index, v, rows8(t), :] = out[v]
            return 0

        lax.fori_loop(0, RT, own_tile, 0, unroll=2)
        exchange(index).start()

    def spread_lists(chunk, _):
        at = pl.ds(pl.multiple_of(chunk * CB, CB), CB)
        lists[pl.ds(chunk * 4, 4), :] = face_nodes[:, at]
        return 0

    lax.fori_loop(0, TILES * 8, spread_lists, 0, unroll=8)

    for chunk in range(8):
        pairs[pl.ds(chunk * 2, 2), :] = inner_cells[:, chunk * CB : (chunk + 1) * CB]

    for d in range(3):
        for h in range(4):
            nodes[6 * d + 1 + h] = jnp.broadcast_to(node_vel[d : d + 1, h * CB : (h + 1) * CB], (8, CB))
    for side in range(2):
        halo_copy(side).wait()
        if remote:
            inside = (dom != n_dom - 1) if side else (dom != 0)
        for d in range(3):
            row = jnp.broadcast_to(halo[side, d : d + 1, :], (8, CB))
            if remote:
                row = jnp.where(inside, row, 0.0)
            nodes[6 * d + 5 * side] = row

    def sweep_tile(tile, _):
        normal = normal_of(tile)
        sums = [None] * 3
        for corner in range(4):
            at = lists[pl.ds(tile * 32 + corner, 8, stride=4), :]
            lanes = at & 127
            chunk = at >> 7
            for d in range(3):
                value = take(nodes[6 * d], lanes)
                for h in range(1, 6):
                    value = jnp.where(chunk == h, take(nodes[6 * d + h], lanes), value)
                sums[d] = value if corner == 0 else sums[d] + value
        sweeps[rows8(tile), :] = (0.25 * STEP_SIZE) * dot3(normal, sums)
        return 0

    lax.fori_loop(0, TILES, sweep_tile, 0)

    total[...] = jnp.zeros_like(total)

    normal = normal_of(0)
    sweep = sweeps[0:8, :]
    left_cells = pairs[pl.ds(0, 8, stride=2), :]
    right_cells = pairs[pl.ds(1, 8, stride=2), :]
    left = rebuild(table, split_cells(left_cells), normal)
    right = rebuild(table, split_cells(right_cells), [-x for x in normal])
    flux = roe_flux(left, right, normal, sweep)
    scatter([-x for x in flux] + [sweep], left_cells, masked.at[0], total)
    scatter(flux + [-sweep], right_cells, masked.at[1], total)

    for index in FLUX_ORDER:
        exchange(index).wait()

        def flux_tile(t, half, index=index):
            tile = 1 + RT * index + t
            ours = [own[index, v, rows8(t), :] for v in range(5)]
            other = [theirs[index, v, rows8(t), :] for v in range(5)]
            sweep = sweeps[rows8(tile), :]
            flux = roe_flux(ours, other, normal_of(tile), sweep)
            scatter([-x for x in flux] + [sweep], cells_of(index, t), masked.at[half], total)

        def flux_pair(t, _):
            flux_tile(2 * t, 0)
            flux_tile(2 * t + 1, 1)
            return 0

        lax.fori_loop(0, RT // 2, flux_pair, 0)

    live = counts[0, 0]
    for h in range(4):
        on = jnp.full((8, CB), h, jnp.int32) < live
        at = pl.ds(h * CB, CB)
        sums = total[h * 12 : h * 12 + 6, :] + total[h * 12 + 6 : h * 12 + 12, :]
        room = volume[0:1, at]
        content[:, at] = room * state[:, at] + jnp.where(on[0:5], STEP_SIZE * sums[0:5, :], 0.0)
        new_volume[0:1, at] = room + jnp.where(on[0:1], sums[5:6, :], 0.0)


def section(remote, state, grad, adjacency, node_vel, face_normal, face_nodes, inner_cells, iface_cells, volume, counts):
    vmem = pl.BlockSpec(memory_space=pltpu.VMEM)
    smem = pl.BlockSpec(memory_space=pltpu.SMEM)
    params = dict(vmem_limit_bytes=60 << 20)
    if remote:
        params.update(collective_id=0, has_side_effects=True)
    return pl.pallas_call(
        functools.partial(kernel, remote),
        out_shape=(
            jax.ShapeDtypeStruct((5, NN), F32),
            jax.ShapeDtypeStruct((1, NN), F32),
        ),
        in_specs=[vmem, vmem, smem, vmem, vmem, vmem, vmem, vmem, vmem, smem],
        out_specs=(vmem, vmem),
        scratch_shapes=[
            pltpu.VMEM((80, 8, CB), F32),
            pltpu.VMEM((18, 8, CB), F32),
            pltpu.VMEM((TILES * 32, CB), F32),
            pltpu.VMEM((TILES * 32, CB), jnp.int32),
            pltpu.VMEM((16, CB), jnp.int32),
            pltpu.VMEM((RT * 64, CB), jnp.int32),
            pltpu.VMEM((ROUNDS, 5, RT * 8, CB), F32),
            pltpu.VMEM((ROUNDS, 5, RT * 8, CB), F32),
            pltpu.VMEM((TILES * 8, CB), F32),
            pltpu.VMEM((2, 3, HN), F32),
            pltpu.VMEM((2, 8 * RS, CB), F32),
            pltpu.VMEM((48, CB), F32),
            pltpu.SemaphoreType.DMA((ROUNDS,)),
            pltpu.SemaphoreType.DMA((ROUNDS,)),
            pltpu.SemaphoreType.DMA((2,)),
            pltpu.SemaphoreType.DMA((2,)),
        ],
        compiler_params=pltpu.CompilerParams(**params),
    )(state, grad, adjacency, node_vel, face_normal, face_nodes, inner_cells, iface_cells, volume, counts)


def shards(
    state,
    grad_op,
    adjacency,
    node_vel,
    face_normal,
    face_nodes,
    inner_cells,
    iface_cells,
    cell_volume,
    block_counts,
):
    content, new_volume = section(
        True,
        state[0, 0],
        grad_op[0, 0],
        adjacency[0, 0],
        node_vel[0, 0],
        face_normal[0, 0],
        face_nodes[0, 0],
        inner_cells[0, 0],
        iface_cells[0, 0],
        cell_volume[0],
        block_counts,
    )
    return (content[None, None], new_volume[None])


def solution(mesh):
    return jax.shard_map(
        shards,
        mesh=mesh,
        in_specs=(
            P("zone", "dom", None, None),
            P("zone", "dom", None, None, None, None),
            P("zone", "dom", None, None),
            P("zone", "dom", None, None),
            P("zone", "dom", None, None),
            P("zone", "dom", None, None),
            P("zone", "dom", None, None),
            P("zone", "dom", None, None),
            P("zone", "dom", None),
            P("zone", "dom"),
        ),
        out_specs=(P("zone", "dom", None, None), P("zone", "dom", None)),
        check_vma=False,
    )
```

time: 686 us -> 36 us (0.05)
  the two profiles are of different devices: /device:TPU:199 before, /device:TPU:1 now
where the time goes in v1:
time: 36 us; the launch traced here: 35.6 us
  Pallas kernels  24.4 us (68%)
  local copies, waits for them, and re-layouts  9.94 us (28%)
  between operations  1.29 us (4%)
    pallas_call x1, Pallas kernels, section(): pl.pallas_call(functools.partial(kernel, remote), out_shape=(jax.ShapeDty...  24.4 us
    unnamed x7, local copies, waits for them, and re-layouts  9.94 us

profile of v1, /device:TPU:1, one launch (start us, length us, event | category | flops | bytes accessed | tf_op | source)
XLA Modules:
  0.0 35.6 jit_solution(16951613692648211316)
XLA Ops:
  1.3 1.3 %copy.12 = s32[1,1,4,3]{3,2,1,0:T(4,128)} copy(s32[1,1,4,3]{2,1,3,0:T(1,128)} %param.12) | data formatting | bytes 96 | tf_op args[2]
  2.6 1.3 %copy.25 = f32[1,1,3,512]{3,2,1,0:T(4,128)} copy(f32[1,1,3,512]{3,1,2,0:T(1,128)} %param.13) | data formatting | bytes 12288
  3.9 1.3 %copy.24 = f32[1,1,5,512]{3,2,1,0:T(8,128)} copy(f32[1,1,5,512]{3,1,2,0:T(1,128)} %param.10) | data formatting | bytes 20480
  5.2 1.6 %copy.23 = s32[1,1,6,4096]{3,2,1,0:T(8,128)} copy(s32[1,1,6,4096]{3,1,2,0:T(1,128)} %param.17) | data formatting | bytes 196608
  6.8 1.8 %copy.22 = f32[1,1,3,25600]{3,2,1,0:T(4,128)} copy(f32[1,1,3,25600]{3,1,2,0:T(1,128)} %param.14) | data formatting | bytes 614400
  8.6 24.4 %shard_map.113 = (f32[5,512]{1,0:T(8,128)}, f32[1,512]{1,0:T(1,128)}) custom-call(f32[5,512]{1,0:T(8,128)} %bitcast.23, bf16[4,3,128,384]{3,2,1,0:T(8,128)(2,1)} %bitcast.20, s32[4,3]{1,0:T(4,128)} %bitcast.27, f32[3,512]{1,0:T(4,128)} %bitcast.24, f32[3,25600]{1,0:T(4,128)} %bitcast.19, s32[4,25600]{1,0:T(4,128)} %bitcast.22, s32[2,1024]{1,0:T(2,128)} %bitcast.26, ...), custom_call_target="tpu_custom_call" | custom-call | tf_op jit(solution)/shard_map/pallas_call | solution.py:384
  33.1 1.3 %copy.13 = f32[1,1,5,512]{3,1,2,0:T(1,128)} copy(f32[1,1,5,512]{3,2,1,0:T(8,128)} %bitcast.25) | data formatting | bytes 20480
  34.4 1.3 %copy.28 = f32[1,1,512]{2,1,0:T(1,128)} copy(f32[1,1,512]{2,1,0:T(1,128)} %bitcast.29) | data formatting | bytes 4096

commit v2 on v1

--- a/solution.py
+++ b/solution.py
@@ -172,22 +172,14 @@
     face_nodes,
     inner_cells,
     iface_cells,
-    volume,
-    counts,
-    content,
-    new_volume,
+    total,
     table,
     nodes,
-    normals,
-    lists,
-    pairs,
-    cells,
     own,
     theirs,
     sweeps,
     halo,
     masked,
-    total,
     send_sem,
     recv_sem,
     halo_send,
@@ -228,7 +220,7 @@
         return pltpu.make_async_copy(own.at[index], theirs.at[index], recv_sem.at[index])
 
     def halo_copy(side):
-        source = node_vel.at[:, pl.ds((NN - HN) * (1 - side), HN)]
+        source = node_vel.at[:, 3 * (1 - side), :]
         if remote:
             return pltpu.make_async_remote_copy(
                 src_ref=source,
@@ -242,14 +234,14 @@
 
     for v in range(5):
         for h in range(4):
-            table[4 * v + h] = jnp.broadcast_to(state[v : v + 1, h * CB : (h + 1) * CB], (8, CB))
+            table[4 * v + h] = jnp.broadcast_to(state[v, h : h + 1, :], (8, CB))
     for b in range(NB):
         sums = None
         for k in range(K):
-            near = jnp.full((5, CB), adjacency[b, k], jnp.int32)
-            block = state[:, 0:CB]
+            near = jnp.full((5, CB), adjacency[k, 0, b], jnp.int32)
+            block = state[:, 0, :]
             for other in range(1, NB):
-                block = jnp.where(near == other, state[:, other * CB : (other + 1) * CB], block)
+                block = jnp.where(near == other, state[:, other, :], block)
             part = jnp.dot(block.astype(BF16), grad[b, k], preferred_element_type=F32)
             sums = part if sums is None else sums + part
         for v in range(5):
@@ -258,25 +250,11 @@
                     sums[v : v + 1, d * CB : (d + 1) * CB], (8, CB)
                 )
 
-    def spread(chunk, _):
-        at = pl.ds(pl.multiple_of(chunk * CB, CB), CB)
-        normals[pl.ds(chunk * 4, 3), :] = face_normal[:, at]
-        return 0
-
-    lax.fori_loop(0, TILES * 8, spread, 0, unroll=8)
-
-    def spread_cells(chunk, _):
-        at = pl.ds(pl.multiple_of(chunk * CB, CB), CB)
-        cells[pl.ds(pl.multiple_of(chunk * 8, 8), ROUNDS), :] = iface_cells[:, at]
-        return 0
-
-    lax.fori_loop(0, RT * 8, spread_cells, 0, unroll=8)
-
     def normal_of(tile):
-        return [normals[pl.ds(tile * 32 + d, 8, stride=4), :] for d in range(3)]
+        return [face_normal[d, rows8(tile), :] for d in range(3)]
 
     def cells_of(index, t):
-        return cells[pl.ds(t * 64 + index, 8, stride=8), :]
+        return iface_cells[index, rows8(t), :]
 
     if remote:
         pl.semaphore_wait(barrier, len(peers) + 2)
@@ -292,22 +270,12 @@
                 own[index, v, rows8(t), :] = out[v]
             return 0
 
-        lax.fori_loop(0, RT, own_tile, 0, unroll=2)
+        lax.fori_loop(0, RT, own_tile, 0, unroll=RT)
         exchange(index).start()
-
-    def spread_lists(chunk, _):
-        at = pl.ds(pl.multiple_of(chunk * CB, CB), CB)
-        lists[pl.ds(chunk * 4, 4), :] = face_nodes[:, at]
-        return 0
-
-    lax.fori_loop(0, TILES * 8, spread_lists, 0, unroll=8)
-
-    for chunk in range(8):
-        pairs[pl.ds(chunk * 2, 2), :] = inner_cells[:, chunk * CB : (chunk + 1) * CB]
 
     for d in range(3):
         for h in range(4):
-            nodes[6 * d + 1 + h] = jnp.broadcast_to(node_vel[d : d + 1, h * CB : (h + 1) * CB], (8, CB))
+            nodes[6 * d + 1 + h] = jnp.broadcast_to(node_vel[d, h : h + 1, :], (8, CB))
     for side in range(2):
         halo_copy(side).wait()
         if remote:
@@ -322,7 +290,7 @@
         normal = normal_of(tile)
         sums = [None] * 3
         for corner in range(4):
-            at = lists[pl.ds(tile * 32 + corner, 8, stride=4), :]
+            at = face_nodes[pl.ds(tile * 32 + corner, 8, stride=4), :]
             lanes = at & 127
             chunk = at >> 7
             for d in range(3):
@@ -333,14 +301,14 @@
         sweeps[rows8(tile), :] = (0.25 * STEP_SIZE) * dot3(normal, sums)
         return 0
 
-    lax.fori_loop(0, TILES, sweep_tile, 0)
+    lax.fori_loop(0, TILES, sweep_tile, 0, unroll=5)
 
     total[...] = jnp.zeros_like(total)
 
     normal = normal_of(0)
     sweep = sweeps[0:8, :]
-    left_cells = pairs[pl.ds(0, 8, stride=2), :]
-    right_cells = pairs[pl.ds(1, 8, stride=2), :]
+    left_cells = inner_cells[pl.ds(0, 8, stride=2), :]
+    right_cells = inner_cells[pl.ds(1, 8, stride=2), :]
     left = rebuild(table, split_cells(left_cells), normal)
     right = rebuild(table, split_cells(right_cells), [-x for x in normal])
     flux = roe_flux(left, right, normal, sweep)
@@ -365,14 +333,15 @@
 
         lax.fori_loop(0, RT // 2, flux_pair, 0)
 
+
+def finish(total, state, volume, counts, content, new_volume):
     live = counts[0, 0]
     for h in range(4):
         on = jnp.full((8, CB), h, jnp.int32) < live
-        at = pl.ds(h * CB, CB)
         sums = total[h * 12 : h * 12 + 6, :] + total[h * 12 + 6 : h * 12 + 12, :]
-        room = volume[0:1, at]
-        content[:, at] = room * state[:, at] + jnp.where(on[0:5], STEP_SIZE * sums[0:5, :], 0.0)
-        new_volume[0:1, at] = room + jnp.where(on[0:1], sums[5:6, :], 0.0)
+        room = volume[h : h + 1, :]
+        content[:, h, :] = room * state[:, h, :] + jnp.where(on[0:5], STEP_SIZE * sums[0:5, :], 0.0)
+        new_volume[h : h + 1, :] = room + jnp.where(on[0:1], sums[5:6, :], 0.0)
 
 
 def section(remote, state, grad, adjacency, node_vel, face_normal, face_nodes, inner_cells, iface_cells, volume, counts):
@@ -381,34 +350,40 @@
     params = dict(vmem_limit_bytes=60 << 20)
     if remote:
         params.update(collective_id=0, has_side_effects=True)
-    return pl.pallas_call(
+    total = pl.pallas_call(
         functools.partial(kernel, remote),
-        out_shape=(
-            jax.ShapeDtypeStruct((5, NN), F32),
-            jax.ShapeDtypeStruct((1, NN), F32),
-        ),
-        in_specs=[vmem, vmem, smem, vmem, vmem, vmem, vmem, vmem, vmem, smem],
-        out_specs=(vmem, vmem),
+        out_shape=jax.ShapeDtypeStruct((48, CB), F32),
+        in_specs=[vmem, vmem, smem, vmem, vmem, vmem, vmem, vmem],
+        out_specs=vmem,
         scratch_shapes=[
             pltpu.VMEM((80, 8, CB), F32),
             pltpu.VMEM((18, 8, CB), F32),
-            pltpu.VMEM((TILES * 32, CB), F32),
-            pltpu.VMEM((TILES * 32, CB), jnp.int32),
-            pltpu.VMEM((16, CB), jnp.int32),
-            pltpu.VMEM((RT * 64, CB), jnp.int32),
             pltpu.VMEM((ROUNDS, 5, RT * 8, CB), F32),
             pltpu.VMEM((ROUNDS, 5, RT * 8, CB), F32),
             pltpu.VMEM((TILES * 8, CB), F32),
             pltpu.VMEM((2, 3, HN), F32),
             pltpu.VMEM((2, 8 * RS, CB), F32),
-            pltpu.VMEM((48, CB), F32),
             pltpu.SemaphoreType.DMA((ROUNDS,)),
             pltpu.SemaphoreType.DMA((ROUNDS,)),
             pltpu.SemaphoreType.DMA((2,)),
             pltpu.SemaphoreType.DMA((2,)),
         ],
         compiler_params=pltpu.CompilerParams(**params),
-    )(state, grad, adjacency, node_vel, face_normal, face_nodes, inner_cells, iface_cells, volume, counts)
+    )(state, grad, adjacency, node_vel, face_normal, face_nodes, inner_cells, iface_cells)
+    return pl.pallas_call(
+        finish,
+        out_shape=(
+            jax.ShapeDtypeStruct((5, NB, CB), F32),
+            jax.ShapeDtypeStruct((NB, CB), F32),
+        ),
+        in_specs=[vmem, vmem, vmem, smem],
+        out_specs=(vmem, vmem),
+    )(total, state, volume, counts)
+
+
+def by_chunk(rows):
+    count, length = rows.shape
+    return rows.reshape(count, length // CB, CB).swapaxes(0, 1).reshape(count * length // CB, CB)
 
 
 def shards(
@@ -425,18 +400,18 @@
 ):
     content, new_volume = section(
         True,
-        state[0, 0],
-        grad_op[0, 0],
-        adjacency[0, 0],
-        node_vel[0, 0],
-        face_normal[0, 0],
-        face_nodes[0, 0],
-        inner_cells[0, 0],
-        iface_cells[0, 0],
-        cell_volume[0],
+        state.reshape(5, NB, CB),
+        grad_op.reshape(NB, K, CB, 3 * CB),
+        jnp.swapaxes(adjacency, 2, 3).reshape(K, 1, NB),
+        node_vel.reshape(3, NB, CB),
+        face_normal.reshape(3, TILES * 8, CB),
+        by_chunk(face_nodes[0, 0]),
+        by_chunk(inner_cells[0, 0]),
+        iface_cells.reshape(ROUNDS, RT * 8, CB),
+        cell_volume.reshape(NB, CB),
         block_counts,
     )
-    return (content[None, None], new_volume[None])
+    return (content.reshape(1, 1, 5, NN), new_volume.reshape(1, 1, NN))
 
 
 def solution(mesh):

time: 36 us -> 28 us (0.78)
  local copies, waits for them, and re-layouts: 9.94 us -> 0 us
  Pallas kernels: 24.4 us -> 26.5 us
    unnamed x7 -> x0, local copies, waits for them, and re-layouts: 9.94 us -> none
    pallas_call x1 -> x2, Pallas kernels: 24.4 us -> 26.5 us  [the longest x1 25.1 us: section(): pl.pallas_call(functools.partial(kernel, remote), out_shape=jax.ShapeDtyp...]
where the time goes in v2:
time: 28 us; the launch traced here: 27.8 us
  Pallas kernels  26.5 us (95%)
  between operations  1.29 us (5%)
    pallas_call x1, Pallas kernels, section(): pl.pallas_call(functools.partial(kernel, remote), out_shape=jax.ShapeDtyp...  25.1 us
    pallas_call x1, Pallas kernels, section(): pl.pallas_call(finish, out_shape=(jax.ShapeDtypeStruct((5, NB, CB), F32),...  1.38 us

profile of v2, /device:TPU:1, one launch (start us, length us, event | category | flops | bytes accessed | tf_op | source)
XLA Modules:
  0.0 27.8 jit_solution(10271520884512447681)
XLA Ops:
  1.3 25.1 %shard_map.113.total = f32[48,128]{1,0:T(8,128)} custom-call(f32[5,4,128]{2,1,0:T(4,128)} %bitcast.25, bf16[4,3,128,384]{3,2,1,0:T(8,128)(2,1)} %bitcast.21, s32[3,1,4]{2,1,0:T(1,128)} %bitcast.30, f32[3,4,128]{2,1,0:T(4,128)} %bitcast.28, f32[3,200,128]{2,1,0:T(8,128)} %bitcast.23, s32[800,128]{1,0:T(8,128)} %bitcast.22, s32[16,128]{1,0:T(8,128)} %bitcast.27, ...), custom_call_target="tpu_custom_call" | custom-call | tf_op jit(solution)/shard_map/pallas_call | solution.py:353
  26.4 1.4 %shard_map.114 = (f32[5,4,128]{2,1,0:T(4,128)}, f32[4,128]{1,0:T(4,128)}) custom-call(f32[48,128]{1,0:T(8,128)} %shard_map.113.total, f32[5,4,128]{2,1,0:T(4,128)} %bitcast.26, f32[4,128]{1,0:T(4,128)} %bitcast.29, s32[1,1]{1,0:T(1,128)S(6)} %copy.18.counts), custom_call_target="tpu_custom_call" | custom-call | tf_op jit(solution)/shard_map/pallas_call | solution.py:373

commit v3 on v2

--- a/solution.py
+++ b/solution.py
@@ -21,8 +21,8 @@
 RECON_GAIN = 0.2
 GAMMA_LESS = 0.4
 
-SEND_ORDER = (2, 1, 5, 4, 3, 0)
-FLUX_ORDER = (2, 1, 5, 4, 3, 0)
+SEND_ORDER = (2, 4, 1, 5, 3, 0)
+FLUX_ORDER = (0, 3, 5, 4, 1, 2)
 
 F32 = jnp.float32
 BF16 = jnp.bfloat16
@@ -164,6 +164,15 @@
 
 def kernel(
     remote,
+    state_hbm,
+    grad_hbm,
+    adjacency_hbm,
+    node_vel_hbm,
+    face_normal_hbm,
+    face_nodes_hbm,
+    inner_cells_hbm,
+    iface_cells_hbm,
+    total,
     state,
     grad,
     adjacency,
@@ -172,7 +181,6 @@
     face_nodes,
     inner_cells,
     iface_cells,
-    total,
     table,
     nodes,
     own,
@@ -184,7 +192,23 @@
     recv_sem,
     halo_send,
     halo_recv,
+    stage_sem,
+    grad_sem,
 ):
+    def stage(source, target, sem):
+        copy = pltpu.make_async_copy(source, target, sem)
+        copy.start()
+        return copy
+
+    staged_state = stage(state_hbm, state, stage_sem.at[0])
+    staged_adjacency = stage(adjacency_hbm, adjacency, stage_sem.at[1])
+    staged_grad = [stage(grad_hbm.at[b], grad.at[b], grad_sem.at[b]) for b in range(NB)]
+    staged_cells = stage(iface_cells_hbm, iface_cells, stage_sem.at[2])
+    staged_normal = stage(face_normal_hbm, face_normal, stage_sem.at[3])
+    staged_vel = stage(node_vel_hbm, node_vel, stage_sem.at[4])
+    staged_pairs = stage(inner_cells_hbm, inner_cells, stage_sem.at[5])
+    staged_nodes = stage(face_nodes_hbm, face_nodes, stage_sem.at[6])
+
     if remote:
         zone = lax.axis_index("zone")
         dom = lax.axis_index("dom")
@@ -232,13 +256,16 @@
             )
         return pltpu.make_async_copy(source, halo.at[side], halo_recv.at[side])
 
+    staged_state.wait()
+    staged_adjacency.wait()
     for v in range(5):
         for h in range(4):
             table[4 * v + h] = jnp.broadcast_to(state[v, h : h + 1, :], (8, CB))
     for b in range(NB):
         sums = None
+        staged_grad[b].wait()
         for k in range(K):
-            near = jnp.full((5, CB), adjacency[k, 0, b], jnp.int32)
+            near = jnp.broadcast_to(adjacency[k, :, b : b + 1], (5, CB))
             block = state[:, 0, :]
             for other in range(1, NB):
                 block = jnp.where(near == other, state[:, other, :], block)
@@ -258,8 +285,12 @@
 
     if remote:
         pl.semaphore_wait(barrier, len(peers) + 2)
+    staged_vel.wait()
     for side in range(2):
         halo_copy(side).start()
+
+    staged_cells.wait()
+    staged_normal.wait()
 
     for index in SEND_ORDER:
 
@@ -285,6 +316,9 @@
             if remote:
                 row = jnp.where(inside, row, 0.0)
             nodes[6 * d + 5 * side] = row
+
+    staged_nodes.wait()
+    staged_pairs.wait()
 
     def sweep_tile(tile, _):
         normal = normal_of(tile)
@@ -301,7 +335,12 @@
         sweeps[rows8(tile), :] = (0.25 * STEP_SIZE) * dot3(normal, sums)
         return 0
 
-    lax.fori_loop(0, TILES, sweep_tile, 0, unroll=5)
+    def first_sweeps(t, _):
+        sweep_tile(1 + RT * FLUX_ORDER[0] + t, 0)
+        return 0
+
+    sweep_tile(0, 0)
+    lax.fori_loop(0, RT, first_sweeps, 0, unroll=RT)
 
     total[...] = jnp.zeros_like(total)
 
@@ -315,7 +354,8 @@
     scatter([-x for x in flux] + [sweep], left_cells, masked.at[0], total)
     scatter(flux + [-sweep], right_cells, masked.at[1], total)
 
-    for index in FLUX_ORDER:
+    for place, index in enumerate(FLUX_ORDER):
+        later = FLUX_ORDER[place + 1] if place + 1 < ROUNDS else None
         exchange(index).wait()
 
         def flux_tile(t, half, index=index):
@@ -326,7 +366,10 @@
             flux = roe_flux(ours, other, normal_of(tile), sweep)
             scatter([-x for x in flux] + [sweep], cells_of(index, t), masked.at[half], total)
 
-        def flux_pair(t, _):
+        def flux_pair(t, _, later=later):
+            if later is not None:
+                for i in range(2):
+                    sweep_tile(1 + RT * later + 2 * t + i, 0)
             flux_tile(2 * t, 0)
             flux_tile(2 * t + 1, 1)
             return 0
@@ -335,9 +378,9 @@
 
 
 def finish(total, state, volume, counts, content, new_volume):
-    live = counts[0, 0]
+    live = jnp.broadcast_to(counts[...], (8, CB))
     for h in range(4):
-        on = jnp.full((8, CB), h, jnp.int32) < live
+        on = live > h
         sums = total[h * 12 : h * 12 + 6, :] + total[h * 12 + 6 : h * 12 + 12, :]
         room = volume[h : h + 1, :]
         content[:, h, :] = room * state[:, h, :] + jnp.where(on[0:5], STEP_SIZE * sums[0:5, :], 0.0)
@@ -346,16 +389,18 @@
 
 def section(remote, state, grad, adjacency, node_vel, face_normal, face_nodes, inner_cells, iface_cells, volume, counts):
     vmem = pl.BlockSpec(memory_space=pltpu.VMEM)
-    smem = pl.BlockSpec(memory_space=pltpu.SMEM)
+    hbm = pl.BlockSpec(memory_space=pltpu.HBM)
     params = dict(vmem_limit_bytes=60 << 20)
     if remote:
         params.update(collective_id=0, has_side_effects=True)
+    inputs = (state, grad, adjacency, node_vel, face_normal, face_nodes, inner_cells, iface_cells)
     total = pl.pallas_call(
         functools.partial(kernel, remote),
         out_shape=jax.ShapeDtypeStruct((48, CB), F32),
-        in_specs=[vmem, vmem, smem, vmem, vmem, vmem, vmem, vmem],
+        in_specs=[hbm] * 8,
         out_specs=vmem,
         scratch_shapes=[
+            *(pltpu.VMEM(x.shape, x.dtype) for x in inputs),
             pltpu.VMEM((80, 8, CB), F32),
             pltpu.VMEM((18, 8, CB), F32),
             pltpu.VMEM((ROUNDS, 5, RT * 8, CB), F32),
@@ -367,16 +412,18 @@
             pltpu.SemaphoreType.DMA((ROUNDS,)),
             pltpu.SemaphoreType.DMA((2,)),
             pltpu.SemaphoreType.DMA((2,)),
+            pltpu.SemaphoreType.DMA((7,)),
+            pltpu.SemaphoreType.DMA((NB,)),
         ],
         compiler_params=pltpu.CompilerParams(**params),
-    )(state, grad, adjacency, node_vel, face_normal, face_nodes, inner_cells, iface_cells)
+    )(*inputs)
     return pl.pallas_call(
         finish,
         out_shape=(
             jax.ShapeDtypeStruct((5, NB, CB), F32),
             jax.ShapeDtypeStruct((NB, CB), F32),
         ),
-        in_specs=[vmem, vmem, vmem, smem],
+        in_specs=[vmem] * 4,
         out_specs=(vmem, vmem),
     )(total, state, volume, counts)
 

time: 28 us -> 22.6 us (0.81)
  the two profiles are of different devices: /device:TPU:1 before, /device:TPU:28 now
where the time goes in v3:
time: 22.6 us; the launch traced here: 22.4 us
  Pallas kernels  21.1 us (93%)
  between operations  1.29 us (6%)
    pallas_call x1, Pallas kernels, section(): pl.pallas_call(functools.partial(kernel, remote), out_shape=jax.ShapeDtyp...  19.7 us
    pallas_call x1, Pallas kernels, section(): pl.pallas_call(finish, out_shape=(jax.ShapeDtypeStruct((5, NB, CB), F32),...  1.44 us

profile of v3, /device:TPU:28, one launch (start us, length us, event | category | flops | bytes accessed | tf_op | source)
XLA Modules:
  0.0 22.4 jit_solution(10933303307541587634)
XLA Ops:
  1.3 19.7 %shard_map.113.total = f32[48,128]{1,0:T(8,128)} custom-call(f32[5,4,128]{2,1,0:T(4,128)} %bitcast.25, bf16[4,3,128,384]{3,2,1,0:T(8,128)(2,1)} %bitcast.21, s32[3,1,4]{2,1,0:T(1,128)} %bitcast.30, f32[3,4,128]{2,1,0:T(4,128)} %bitcast.28, f32[3,200,128]{2,1,0:T(8,128)} %bitcast.23, s32[800,128]{1,0:T(8,128)} %bitcast.22, s32[16,128]{1,0:T(8,128)} %bitcast.27, ...), custom_call_target="tpu_custom_call" | custom-call | tf_op jit(solution)/shard_map/pallas_call | solution.py:397
  21.0 1.4 %shard_map.114 = (f32[5,4,128]{2,1,0:T(4,128)}, f32[4,128]{1,0:T(4,128)}) custom-call(f32[48,128]{1,0:T(8,128)} %shard_map.113.total, f32[5,4,128]{2,1,0:T(4,128)} %bitcast.26, f32[4,128]{1,0:T(4,128)} %bitcast.29, s32[1,1]{1,0:T(1,128)S(6)} %copy.18.counts), custom_call_target="tpu_custom_call" | custom-call | tf_op jit(solution)/shard_map/pallas_call | solution.py:420

commit v4 on v3

--- a/solution.py
+++ b/solution.py
@@ -15,7 +15,7 @@
 NN = 512
 RT = 4
 TILES = 25
-RS = 56
+RS = 24
 
 STEP_SIZE = 0.25
 RECON_GAIN = 0.2
@@ -23,6 +23,11 @@
 
 SEND_ORDER = (2, 4, 1, 5, 3, 0)
 FLUX_ORDER = (0, 3, 5, 4, 1, 2)
+
+REST_AFTER = 1
+LATE_HOLDS = (4, 1)
+CROSSING = 2
+VMEM_LIMIT = 60 << 20
 
 F32 = jnp.float32
 BF16 = jnp.bfloat16
@@ -141,22 +146,25 @@
     return [scale * x for x in out]
 
 
-def scatter(terms, where_cells, masked, total):
-    lanes = where_cells & 127
-    chunk = where_cells >> 7
+def scatter(terms, where_cells, split, total):
     for v, x in enumerate(terms):
         upper = x.astype(BF16).astype(F32)
-        for piece, part in enumerate((upper, x - upper)):
-            for h in range(4):
-                masked[pl.ds(h * 12 + piece * 6 + v, 8, stride=RS), :] = jnp.where(chunk == h, part, 0.0)
-    slot = lax.broadcasted_iota(jnp.int32, (128, 128), 0)
+        split[pl.ds(v, 8, stride=RS), :] = upper
+        split[pl.ds(v + 6, 8, stride=RS), :] = x - upper
+    lanes = (where_cells & 127).astype(F32)
+    chunk = (where_cells >> 7).astype(F32)
+    slot = lax.broadcasted_iota(jnp.int32, (CB, CB), 0).astype(F32).astype(BF16)
+    one, zero = jnp.ones((), BF16), jnp.zeros((), BF16)
     result = None
     for s in range(0, 8, 2):
-        pair = (s, s + 1)
-        left = jnp.concatenate([masked[i * RS : i * RS + 48, :].astype(BF16) for i in pair], axis=1)
-        right = jnp.concatenate(
-            [jnp.where(lanes[i : i + 1, :] == slot, 1.0, 0.0).astype(BF16) for i in pair], axis=1
-        )
+        left, right = [], []
+        for i in (s, s + 1):
+            rows = split[i * RS : i * RS + 16, :].astype(BF16)
+            home = jnp.broadcast_to(chunk[i : i + 1, :], (16, CB)).astype(BF16)
+            left.append(jnp.concatenate([jnp.where(home == h, rows, zero) for h in range(4)], axis=0))
+            at = jnp.broadcast_to(lanes[i : i + 1, :], (CB, CB)).astype(BF16)
+            right.append(jnp.where(at == slot, one, zero))
+        left, right = jnp.concatenate(left, axis=1), jnp.concatenate(right, axis=1)
         part = lax.dot_general(left, right, (((1,), (1,)), ((), ())), preferred_element_type=F32)
         result = part if result is None else result + part
     total[...] += result
@@ -187,27 +195,46 @@
     theirs,
     sweeps,
     halo,
-    masked,
+    split,
     send_sem,
     recv_sem,
     halo_send,
     halo_recv,
     stage_sem,
     grad_sem,
+    ready,
 ):
     def stage(source, target, sem):
         copy = pltpu.make_async_copy(source, target, sem)
         copy.start()
         return copy
 
+    halo[...] = jnp.zeros_like(halo)
+    first = SEND_ORDER[0]
+    top, bottom = 8 * (1 + RT * first), 8 * (1 + RT * (first + 1))
+
+    def piece(source, target, at, sem):
+        return stage(source.at[at], target.at[at], sem)
+
     staged_state = stage(state_hbm, state, stage_sem.at[0])
     staged_adjacency = stage(adjacency_hbm, adjacency, stage_sem.at[1])
     staged_grad = [stage(grad_hbm.at[b], grad.at[b], grad_sem.at[b]) for b in range(NB)]
-    staged_cells = stage(iface_cells_hbm, iface_cells, stage_sem.at[2])
-    staged_normal = stage(face_normal_hbm, face_normal, stage_sem.at[3])
-    staged_vel = stage(node_vel_hbm, node_vel, stage_sem.at[4])
-    staged_pairs = stage(inner_cells_hbm, inner_cells, stage_sem.at[5])
-    staged_nodes = stage(face_nodes_hbm, face_nodes, stage_sem.at[6])
+    staged_first = [
+        piece(iface_cells_hbm, iface_cells, pl.ds(first, 1), stage_sem.at[2]),
+        piece(face_normal_hbm, face_normal, (slice(None), pl.ds(top, bottom - top)), stage_sem.at[3]),
+    ]
+
+    def stage_rest():
+        return [
+            piece(iface_cells_hbm, iface_cells, pl.ds(first + 1, ROUNDS - first - 1), stage_sem.at[4]),
+            piece(face_normal_hbm, face_normal, (slice(None), pl.ds(bottom, TILES * 8 - bottom)), stage_sem.at[5]),
+            piece(iface_cells_hbm, iface_cells, pl.ds(0, first), stage_sem.at[6]),
+            piece(face_normal_hbm, face_normal, (slice(None), pl.ds(0, top)), stage_sem.at[7]),
+        ], [
+            stage(node_vel_hbm, node_vel, stage_sem.at[8]),
+            stage(inner_cells_hbm, inner_cells, stage_sem.at[9]),
+            stage(face_nodes_hbm, face_nodes, stage_sem.at[10]),
+        ]
 
     if remote:
         zone = lax.axis_index("zone")
@@ -215,6 +242,8 @@
         n_dom = lax.axis_size("dom")
         nxt = lax.rem(dom + 1, n_dom)
         prv = lax.rem(dom + n_dom - 1, n_dom)
+        has_nxt = 1 - (dom + 1) // n_dom
+        has_prv = 1 - (n_dom - dom) // n_dom
 
         def flip(at, bit):
             return at + bit * (1 - 2 * ((at // bit) % 2))
@@ -227,24 +256,51 @@
             (flip(zone, 1), dom),
             (zone, flip(dom, 16)),
         ]
+        def is_late(at):
+            return (at // 4) % 2
+
+        late = is_late(dom)
+        early = 1 - late
+        late_nxt = is_late(nxt)
+        late_prv = is_late(prv)
+
+        def signal(sem, peer):
+            pl.semaphore_signal(sem, inc=1, device_id=peer, device_id_type=pl.DeviceIdType.MESH)
+
         barrier = pltpu.get_barrier_semaphore()
-        for peer in peers + [(zone, nxt), (zone, prv)]:
-            pl.semaphore_signal(barrier, inc=1, device_id=peer, device_id_type=pl.DeviceIdType.MESH)
-
-    def exchange(index):
+        for index in (4, 1, 0, 3, 5):
+            signal(barrier, peers[index])
+
+        @pl.when(early == 1)
+        def _():
+            signal(barrier, peers[2])
+
+        @pl.when(has_nxt * (early + late_nxt) > 0)
+        def _():
+            signal(barrier, (zone, nxt))
+
+        @pl.when(has_prv * (early + late_prv) > 0)
+        def _():
+            signal(barrier, (zone, prv))
+
+    def exchange(index, half=None):
+        if half is None:
+            at, sem = pl.ds(2 * index, 2), 2 * index
+        else:
+            at = sem = 2 * index + half
         if remote:
             return pltpu.make_async_remote_copy(
-                src_ref=own.at[index],
-                dst_ref=theirs.at[index],
-                send_sem=send_sem.at[index],
-                recv_sem=recv_sem.at[index],
+                src_ref=own.at[at],
+                dst_ref=theirs.at[at],
+                send_sem=send_sem.at[sem],
+                recv_sem=recv_sem.at[sem],
                 device_id=peers[index],
                 device_id_type=pl.DeviceIdType.MESH,
             )
-        return pltpu.make_async_copy(own.at[index], theirs.at[index], recv_sem.at[index])
+        return pltpu.make_async_copy(own.at[at], theirs.at[at], recv_sem.at[sem])
 
     def halo_copy(side):
-        source = node_vel.at[:, 3 * (1 - side), :]
+        source = node_vel_hbm.at[:, 3 * (1 - side), :]
         if remote:
             return pltpu.make_async_remote_copy(
                 src_ref=source,
@@ -256,6 +312,57 @@
             )
         return pltpu.make_async_copy(source, halo.at[side], halo_recv.at[side])
 
+    def enter():
+        meet_nxt = has_nxt * (1 - early * late_nxt)
+        meet_prv = has_prv * (1 - early * late_prv)
+        pl.semaphore_wait(barrier, 5 + late + meet_nxt + meet_prv)
+
+        @pl.when(late == 1)
+        def _():
+            signal(ready.at[0], peers[2])
+
+        @pl.when(late * (1 - late_nxt) * has_nxt == 1)
+        def _():
+            signal(ready.at[1], (zone, nxt))
+
+        @pl.when(late * (1 - late_prv) * has_prv == 1)
+        def _():
+            signal(ready.at[2], (zone, prv))
+
+        @pl.when(meet_nxt == 1)
+        def _():
+            halo_copy(0).start()
+
+        @pl.when(meet_prv == 1)
+        def _():
+            halo_copy(1).start()
+
+    def cross(what):
+        if what == 0:
+
+            @pl.when(early * late_nxt * has_nxt == 1)
+            def _():
+                pl.semaphore_wait(ready.at[2], 1)
+                halo_copy(0).start()
+
+        elif what == 1:
+
+            @pl.when(early * late_prv * has_prv == 1)
+            def _():
+                pl.semaphore_wait(ready.at[1], 1)
+                halo_copy(1).start()
+
+        else:
+
+            @pl.when(early == 1)
+            def _():
+                pl.semaphore_wait(ready.at[0], 1)
+                for half in range(2):
+                    exchange(CROSSING, half).start()
+
+    if remote:
+        pl.when(late == 1)(enter)
+
     staged_state.wait()
     staged_adjacency.wait()
     for v in range(5):
@@ -264,6 +371,8 @@
     for b in range(NB):
         sums = None
         staged_grad[b].wait()
+        if b == REST_AFTER:
+            staged_faces, staged_late = stage_rest()
         for k in range(K):
             near = jnp.broadcast_to(adjacency[k, :, b : b + 1], (5, CB))
             block = state[:, 0, :]
@@ -284,65 +393,112 @@
         return iface_cells[index, rows8(t), :]
 
     if remote:
-        pl.semaphore_wait(barrier, len(peers) + 2)
-    staged_vel.wait()
-    for side in range(2):
-        halo_copy(side).start()
-
-    staged_cells.wait()
-    staged_normal.wait()
+        pl.when(early == 1)(enter)
+    else:
+        for side in range(2):
+            halo_copy(side).start()
+
+    for copy in staged_first:
+        copy.wait()
 
     for index in SEND_ORDER:
-
-        def own_tile(t, _, index=index):
-            where = split_cells(cells_of(index, t))
-            out = rebuild(table, where, normal_of(1 + RT * index + t))
-            for v in range(5):
-                own[index, v, rows8(t), :] = out[v]
-            return 0
-
-        lax.fori_loop(0, RT, own_tile, 0, unroll=RT)
-        exchange(index).start()
+        if index == SEND_ORDER[1]:
+            for copy in staged_faces:
+                copy.wait()
+
+        for half in range(2):
+            for t in range(2):
+                tile = 2 * half + t
+                where = split_cells(cells_of(index, tile))
+                out = rebuild(table, where, normal_of(1 + RT * index + tile))
+                for v in range(5):
+                    own[2 * index + half, v, rows8(t), :] = out[v]
+            if index == CROSSING:
+                if remote:
+
+                    @pl.when(late == 1)
+                    def _(half=half):
+                        exchange(CROSSING, half).start()
+
+                else:
+                    exchange(index, half).start()
+        if remote and index in LATE_HOLDS:
+
+            @pl.when(late == 0)
+            def _(index=index):
+                exchange(index).start()
+
+        elif index != CROSSING:
+            exchange(index).start()
+
+    if remote:
+
+        @pl.when(late == 1)
+        def _():
+            for index in LATE_HOLDS:
+                exchange(index).start()
+
+    for copy in staged_late:
+        copy.wait()
 
     for d in range(3):
         for h in range(4):
             nodes[6 * d + 1 + h] = jnp.broadcast_to(node_vel[d, h : h + 1, :], (8, CB))
-    for side in range(2):
-        halo_copy(side).wait()
-        if remote:
-            inside = (dom != n_dom - 1) if side else (dom != 0)
-        for d in range(3):
-            row = jnp.broadcast_to(halo[side, d : d + 1, :], (8, CB))
-            if remote:
-                row = jnp.where(inside, row, 0.0)
-            nodes[6 * d + 5 * side] = row
-
-    staged_nodes.wait()
-    staged_pairs.wait()
-
-    def sweep_tile(tile, _):
-        normal = normal_of(tile)
-        sums = [None] * 3
+
+    def corners(tile):
         for corner in range(4):
             at = face_nodes[pl.ds(tile * 32 + corner, 8, stride=4), :]
-            lanes = at & 127
-            chunk = at >> 7
+            yield at & 127, at >> 7
+
+    def inner_sweep(tile):
+        sums = [0.0] * 3
+        for lanes, chunk in corners(tile):
+            masks = [chunk == h for h in range(1, 5)]
             for d in range(3):
-                value = take(nodes[6 * d], lanes)
-                for h in range(1, 6):
-                    value = jnp.where(chunk == h, take(nodes[6 * d + h], lanes), value)
-                sums[d] = value if corner == 0 else sums[d] + value
-        sweeps[rows8(tile), :] = (0.25 * STEP_SIZE) * dot3(normal, sums)
+                value = 0.0
+                for h in range(1, 5):
+                    value = jnp.where(masks[h - 1], take(nodes[6 * d + h], lanes), value)
+                sums[d] = sums[d] + value
+        sweeps[rows8(tile), :] = dot3(normal_of(tile), sums)
+
+    def outer_sweep(tile):
+        sums = [0.0] * 3
+        for lanes, chunk in corners(tile):
+            below, above = chunk == 0, chunk == 5
+            for d in range(3):
+                value = jnp.where(below, take(nodes[6 * d], lanes), 0.0)
+                sums[d] = sums[d] + jnp.where(above, take(nodes[6 * d + 5], lanes), value)
+        total = sweeps[rows8(tile), :] + dot3(normal_of(tile), sums)
+        sweeps[rows8(tile), :] = (0.25 * STEP_SIZE) * total
+
+    def inner_tiles(t, _):
+        for i in range(5):
+            inner_sweep(5 * t + i)
         return 0
 
-    def first_sweeps(t, _):
-        sweep_tile(1 + RT * FLUX_ORDER[0] + t, 0)
-        return 0
-
-    sweep_tile(0, 0)
-    lax.fori_loop(0, RT, first_sweeps, 0, unroll=RT)
+    lax.fori_loop(0, TILES // 5, inner_tiles, 0)
+
+    for side in range(2):
+        if remote:
+            receives = has_nxt if side else has_prv
+
+            @pl.when(receives == 1)
+            def _(side=side):
+                halo_copy(side).wait_recv()
+
+        else:
+            halo_copy(side).wait()
+        for d in range(3):
+            nodes[6 * d + 5 * side] = jnp.broadcast_to(halo[side, d : d + 1, :], (8, CB))
+    if remote:
+        for what in range(3):
+            cross(what)
+
+    for tile in [0] + [1 + RT * FLUX_ORDER[0] + t for t in range(RT)]:
+        outer_sweep(tile)
 
     total[...] = jnp.zeros_like(total)
+    split[...] = jnp.zeros_like(split)
 
     normal = normal_of(0)
     sweep = sweeps[0:8, :]
@@ -351,37 +507,52 @@
     left = rebuild(table, split_cells(left_cells), normal)
     right = rebuild(table, split_cells(right_cells), [-x for x in normal])
     flux = roe_flux(left, right, normal, sweep)
-    scatter([-x for x in flux] + [sweep], left_cells, masked.at[0], total)
-    scatter(flux + [-sweep], right_cells, masked.at[1], total)
+    scatter([-x for x in flux] + [sweep], left_cells, split.at[0], total)
+    scatter(flux + [-sweep], right_cells, split.at[1], total)
 
     for place, index in enumerate(FLUX_ORDER):
         later = FLUX_ORDER[place + 1] if place + 1 < ROUNDS else None
-        exchange(index).wait()
-
-        def flux_tile(t, half, index=index):
-            tile = 1 + RT * index + t
-            ours = [own[index, v, rows8(t), :] for v in range(5)]
-            other = [theirs[index, v, rows8(t), :] for v in range(5)]
+
+        def flux_tile(pair, half, index=index):
+            tile = 1 + RT * index + 2 * pair + half
+            ours = [own[2 * index + pair, v, rows8(half), :] for v in range(5)]
+            other = [theirs[2 * index + pair, v, rows8(half), :] for v in range(5)]
             sweep = sweeps[rows8(tile), :]
             flux = roe_flux(ours, other, normal_of(tile), sweep)
-            scatter([-x for x in flux] + [sweep], cells_of(index, t), masked.at[half], total)
-
-        def flux_pair(t, _, later=later):
+            scatter([-x for x in flux] + [sweep], cells_of(index, 2 * pair + half), split.at[half], total)
+
+        def flux_pair(pair, _, later=later):
             if later is not None:
                 for i in range(2):
-                    sweep_tile(1 + RT * later + 2 * t + i, 0)
-            flux_tile(2 * t, 0)
-            flux_tile(2 * t + 1, 1)
+                    outer_sweep(1 + RT * later + 2 * pair + i)
+            flux_tile(pair, 0)
+            flux_tile(pair, 1)
             return 0
 
-        lax.fori_loop(0, RT // 2, flux_pair, 0)
+        if index == CROSSING:
+            for pair in range(2):
+                exchange(CROSSING, pair).wait()
+                flux_pair(pair, 0)
+        else:
+            exchange(index).wait()
+            lax.fori_loop(0, RT // 2, flux_pair, 0)
+
+    if remote:
+
+        @pl.when(has_nxt == 1)
+        def _():
+            halo_copy(0).wait_send()
+
+        @pl.when(has_prv == 1)
+        def _():
+            halo_copy(1).wait_send()
 
 
 def finish(total, state, volume, counts, content, new_volume):
     live = jnp.broadcast_to(counts[...], (8, CB))
     for h in range(4):
         on = live > h
-        sums = total[h * 12 : h * 12 + 6, :] + total[h * 12 + 6 : h * 12 + 12, :]
+        sums = total[h * 16 : h * 16 + 6, :] + total[h * 16 + 6 : h * 16 + 12, :]
         room = volume[h : h + 1, :]
         content[:, h, :] = room * state[:, h, :] + jnp.where(on[0:5], STEP_SIZE * sums[0:5, :], 0.0)
         new_volume[h : h + 1, :] = room + jnp.where(on[0:1], sums[5:6, :], 0.0)
@@ -390,30 +561,31 @@
 def section(remote, state, grad, adjacency, node_vel, face_normal, face_nodes, inner_cells, iface_cells, volume, counts):
     vmem = pl.BlockSpec(memory_space=pltpu.VMEM)
     hbm = pl.BlockSpec(memory_space=pltpu.HBM)
-    params = dict(vmem_limit_bytes=60 << 20)
+    params = dict(vmem_limit_bytes=VMEM_LIMIT)
     if remote:
         params.update(collective_id=0, has_side_effects=True)
     inputs = (state, grad, adjacency, node_vel, face_normal, face_nodes, inner_cells, iface_cells)
     total = pl.pallas_call(
         functools.partial(kernel, remote),
-        out_shape=jax.ShapeDtypeStruct((48, CB), F32),
+        out_shape=jax.ShapeDtypeStruct((64, CB), F32),
         in_specs=[hbm] * 8,
         out_specs=vmem,
         scratch_shapes=[
             *(pltpu.VMEM(x.shape, x.dtype) for x in inputs),
             pltpu.VMEM((80, 8, CB), F32),
             pltpu.VMEM((18, 8, CB), F32),
-            pltpu.VMEM((ROUNDS, 5, RT * 8, CB), F32),
-            pltpu.VMEM((ROUNDS, 5, RT * 8, CB), F32),
+            pltpu.VMEM((2 * ROUNDS, 5, RT * 4, CB), F32),
+            pltpu.VMEM((2 * ROUNDS, 5, RT * 4, CB), F32),
             pltpu.VMEM((TILES * 8, CB), F32),
             pltpu.VMEM((2, 3, HN), F32),
             pltpu.VMEM((2, 8 * RS, CB), F32),
-            pltpu.SemaphoreType.DMA((ROUNDS,)),
-            pltpu.SemaphoreType.DMA((ROUNDS,)),
+            pltpu.SemaphoreType.DMA((2 * ROUNDS,)),
+            pltpu.SemaphoreType.DMA((2 * ROUNDS,)),
             pltpu.SemaphoreType.DMA((2,)),
             pltpu.SemaphoreType.DMA((2,)),
-            pltpu.SemaphoreType.DMA((7,)),
+            pltpu.SemaphoreType.DMA((11,)),
             pltpu.SemaphoreType.DMA((NB,)),
+            pltpu.SemaphoreType.REGULAR((3,)),
         ],
         compiler_params=pltpu.CompilerParams(**params),
     )(*inputs)

time: 22.6 us -> 21.2 us (0.938)
  the two profiles are of different devices: /device:TPU:28 before, /device:TPU:32 now
where the time goes in v4:
time: 21.2 us; the launch traced here: 21 us
  Pallas kernels  19.8 us (93%)
  between operations  1.29 us (6%)
    pallas_call x1, Pallas kernels, section(): pl.pallas_call(functools.partial(kernel, remote), out_shape=jax.ShapeDtyp...  18.3 us
    pallas_call x1, Pallas kernels, section(): pl.pallas_call(finish, out_shape=(jax.ShapeDtypeStruct((5, NB, CB), F32),...  1.46 us

profile of v4, /device:TPU:32, one launch (start us, length us, event | category | flops | bytes accessed | tf_op | source)
XLA Modules:
  0.0 21.0 jit_solution(472965114820677891)
XLA Ops:
  1.3 18.3 %shard_map.113.total = f32[64,128]{1,0:T(8,128)} custom-call(f32[5,4,128]{2,1,0:T(4,128)} %bitcast.25, bf16[4,3,128,384]{3,2,1,0:T(8,128)(2,1)} %bitcast.21, s32[3,1,4]{2,1,0:T(1,128)} %bitcast.30, f32[3,4,128]{2,1,0:T(4,128)} %bitcast.28, f32[3,200,128]{2,1,0:T(8,128)} %bitcast.23, s32[800,128]{1,0:T(8,128)} %bitcast.22, s32[16,128]{1,0:T(8,128)} %bitcast.27, ...), custom_call_target="tpu_custom_call" | custom-call | tf_op jit(solution)/shard_map/pallas_call | solution.py:568
  19.6 1.5 %shard_map.114 = (f32[5,4,128]{2,1,0:T(4,128)}, f32[4,128]{1,0:T(4,128)}) custom-call(f32[64,128]{1,0:T(8,128)} %shard_map.113.total, f32[5,4,128]{2,1,0:T(4,128)} %bitcast.26, f32[4,128]{1,0:T(4,128)} %bitcast.29, s32[1,1]{1,0:T(1,128)S(6)} %copy.18.counts), custom_call_target="tpu_custom_call" | custom-call | tf_op jit(solution)/shard_map/pallas_call | solution.py:592

commit v5 on v4

--- a/solution.py
+++ b/solution.py
@@ -21,12 +21,14 @@
 RECON_GAIN = 0.2
 GAMMA_LESS = 0.4
 
-SEND_ORDER = (2, 4, 1, 5, 3, 0)
-FLUX_ORDER = (0, 3, 5, 4, 1, 2)
+LATE_ORDER = (2, 5, 3, 0, 4, 1)
+EARLY_ORDER = (1, 4, 5, 3, 0, 2)
+FLUX_ORDER = (0, 3, 5, 4)
 
 REST_AFTER = 1
-LATE_HOLDS = (4, 1)
 CROSSING = 2
+HELD = 1
+HOLD = 3
 VMEM_LIMIT = 60 << 20
 
 F32 = jnp.float32
@@ -210,30 +212,19 @@
         return copy
 
     halo[...] = jnp.zeros_like(halo)
-    first = SEND_ORDER[0]
-    top, bottom = 8 * (1 + RT * first), 8 * (1 + RT * (first + 1))
-
-    def piece(source, target, at, sem):
-        return stage(source.at[at], target.at[at], sem)
-
     staged_state = stage(state_hbm, state, stage_sem.at[0])
     staged_adjacency = stage(adjacency_hbm, adjacency, stage_sem.at[1])
     staged_grad = [stage(grad_hbm.at[b], grad.at[b], grad_sem.at[b]) for b in range(NB)]
     staged_first = [
-        piece(iface_cells_hbm, iface_cells, pl.ds(first, 1), stage_sem.at[2]),
-        piece(face_normal_hbm, face_normal, (slice(None), pl.ds(top, bottom - top)), stage_sem.at[3]),
+        stage(iface_cells_hbm, iface_cells, stage_sem.at[2]),
+        stage(face_normal_hbm, face_normal, stage_sem.at[3]),
     ]
 
     def stage_rest():
         return [
-            piece(iface_cells_hbm, iface_cells, pl.ds(first + 1, ROUNDS - first - 1), stage_sem.at[4]),
-            piece(face_normal_hbm, face_normal, (slice(None), pl.ds(bottom, TILES * 8 - bottom)), stage_sem.at[5]),
-            piece(iface_cells_hbm, iface_cells, pl.ds(0, first), stage_sem.at[6]),
-            piece(face_normal_hbm, face_normal, (slice(None), pl.ds(0, top)), stage_sem.at[7]),
-        ], [
-            stage(node_vel_hbm, node_vel, stage_sem.at[8]),
-            stage(inner_cells_hbm, inner_cells, stage_sem.at[9]),
-            stage(face_nodes_hbm, face_nodes, stage_sem.at[10]),
+            stage(node_vel_hbm, node_vel, stage_sem.at[4]),
+            stage(inner_cells_hbm, inner_cells, stage_sem.at[5]),
+            stage(face_nodes_hbm, face_nodes, stage_sem.at[6]),
         ]
 
     if remote:
@@ -353,8 +344,9 @@
                 halo_copy(1).start()
 
         else:
-
-            @pl.when(early == 1)
+            mixed = late_nxt * has_nxt + late_prv * has_prv
+
+            @pl.when(early * (mixed if what == 2 else 1 - mixed) == 1)
             def _():
                 pl.semaphore_wait(ready.at[0], 1)
                 for half in range(2):
@@ -372,7 +364,7 @@
         sums = None
         staged_grad[b].wait()
         if b == REST_AFTER:
-            staged_faces, staged_late = stage_rest()
+            staged_late = stage_rest()
         for k in range(K):
             near = jnp.broadcast_to(adjacency[k, :, b : b + 1], (5, CB))
             block = state[:, 0, :]
@@ -401,11 +393,9 @@
     for copy in staged_first:
         copy.wait()
 
-    for index in SEND_ORDER:
-        if index == SEND_ORDER[1]:
-            for copy in staged_faces:
-                copy.wait()
-
+    for place in range(ROUNDS):
+        late_index, early_index = LATE_ORDER[place], EARLY_ORDER[place]
+        index = late_index * late + early_index * (1 - late) if remote else late_index
         for half in range(2):
             for t in range(2):
                 tile = 2 * half + t
@@ -413,7 +403,7 @@
                 out = rebuild(table, where, normal_of(1 + RT * index + tile))
                 for v in range(5):
                     own[2 * index + half, v, rows8(t), :] = out[v]
-            if index == CROSSING:
+            if late_index == CROSSING:
                 if remote:
 
                     @pl.when(late == 1)
@@ -421,22 +411,26 @@
                         exchange(CROSSING, half).start()
 
                 else:
-                    exchange(index, half).start()
-        if remote and index in LATE_HOLDS:
-
-            @pl.when(late == 0)
-            def _(index=index):
-                exchange(index).start()
-
-        elif index != CROSSING:
-            exchange(index).start()
-
-    if remote:
-
-        @pl.when(late == 1)
-        def _():
-            for index in LATE_HOLDS:
-                exchange(index).start()
+                    exchange(CROSSING, half).start()
+        if remote:
+            if late_index not in (CROSSING, HELD):
+
+                @pl.when(late == 1)
+                def _(index=late_index):
+                    exchange(index).start()
+
+            if early_index != CROSSING:
+
+                @pl.when(late == 0)
+                def _(index=early_index):
+                    for half in (0, 1) if index == HELD else (None,):
+                        exchange(index, half).start()
+
+        elif late_index == HELD:
+            for half in range(2):
+                exchange(HELD, half).start()
+        elif late_index != CROSSING:
+            exchange(late_index).start()
 
     for copy in staged_late:
         copy.wait()
@@ -476,7 +470,15 @@
             inner_sweep(5 * t + i)
         return 0
 
-    lax.fori_loop(0, TILES // 5, inner_tiles, 0)
+    lax.fori_loop(0, HOLD, inner_tiles, 0)
+    if remote:
+
+        @pl.when(late == 1)
+        def _():
+            for half in range(2):
+                exchange(HELD, half).start()
+
+    lax.fori_loop(HOLD, TILES // 5, inner_tiles, 0)
 
     for side in range(2):
         if remote:
@@ -510,8 +512,18 @@
     scatter([-x for x in flux] + [sweep], left_cells, split.at[0], total)
     scatter(flux + [-sweep], right_cells, split.at[1], total)
 
-    for place, index in enumerate(FLUX_ORDER):
-        later = FLUX_ORDER[place + 1] if place + 1 < ROUNDS else None
+    early_order, late_order = FLUX_ORDER + (HELD, CROSSING), FLUX_ORDER + (CROSSING, HELD)
+
+    def at_place(place):
+        if not remote or early_order[place] == late_order[place]:
+            return early_order[place]
+        return late_order[place] * late + early_order[place] * (1 - late)
+
+    for place in range(ROUNDS):
+        index = at_place(place)
+        later = at_place(place + 1) if place + 1 < ROUNDS else None
+        if remote and place == 1:
+            cross(3)
 
         def flux_tile(pair, half, index=index):
             tile = 1 + RT * index + 2 * pair + half
@@ -529,9 +541,17 @@
             flux_tile(pair, 1)
             return 0
 
-        if index == CROSSING:
+        if early_order[place] in (HELD, CROSSING):
             for pair in range(2):
-                exchange(CROSSING, pair).wait()
+                if remote:
+                    for side, order in ((0, early_order), (1, late_order)):
+
+                        @pl.when(late == side)
+                        def _(index=order[place], pair=pair):
+                            exchange(index, pair).wait()
+
+                else:
+                    exchange(index, pair).wait()
                 flux_pair(pair, 0)
         else:
             exchange(index).wait()
@@ -583,7 +603,7 @@
             pltpu.SemaphoreType.DMA((2 * ROUNDS,)),
             pltpu.SemaphoreType.DMA((2,)),
             pltpu.SemaphoreType.DMA((2,)),
-            pltpu.SemaphoreType.DMA((11,)),
+            pltpu.SemaphoreType.DMA((7,)),
             pltpu.SemaphoreType.DMA((NB,)),
             pltpu.SemaphoreType.REGULAR((3,)),
         ],

time: 21.2 us -> 20.8 us (0.981)
  the two profiles are of different devices: /device:TPU:32 before, /device:TPU:199 now
where the time goes in v5:
time: 20.8 us; the launch traced here: 20.6 us
  Pallas kernels  19.3 us (93%)
  between operations  1.29 us (6%)
    pallas_call x1, Pallas kernels, section(): pl.pallas_call(functools.partial(kernel, remote), out_shape=jax.ShapeDtyp...  17.9 us
    pallas_call x1, Pallas kernels, section(): pl.pallas_call(finish, out_shape=(jax.ShapeDtypeStruct((5, NB, CB), F32),...  1.46 us

profile of v5, /device:TPU:199, one launch (start us, length us, event | category | flops | bytes accessed | tf_op | source)
XLA Modules:
  0.0 20.6 jit_solution(13340855086346478672)
XLA Ops:
  1.3 17.9 %shard_map.113.total = f32[64,128]{1,0:T(8,128)} custom-call(f32[5,4,128]{2,1,0:T(4,128)} %bitcast.25, bf16[4,3,128,384]{3,2,1,0:T(8,128)(2,1)} %bitcast.21, s32[3,1,4]{2,1,0:T(1,128)} %bitcast.30, f32[3,4,128]{2,1,0:T(4,128)} %bitcast.28, f32[3,200,128]{2,1,0:T(8,128)} %bitcast.23, s32[800,128]{1,0:T(8,128)} %bitcast.22, s32[16,128]{1,0:T(8,128)} %bitcast.27, ...), custom_call_target="tpu_custom_call" | custom-call | tf_op jit(solution)/shard_map/pallas_call | solution.py:588
  19.1 1.5 %shard_map.114 = (f32[5,4,128]{2,1,0:T(4,128)}, f32[4,128]{1,0:T(4,128)}) custom-call(f32[64,128]{1,0:T(8,128)} %shard_map.113.total, f32[5,4,128]{2,1,0:T(4,128)} %bitcast.26, f32[4,128]{1,0:T(4,128)} %bitcast.29, s32[1,1]{1,0:T(1,128)S(6)} %copy.18.counts), custom_call_target="tpu_custom_call" | custom-call | tf_op jit(solution)/shard_map/pallas_call | solution.py:612

commit v6 on v5

--- a/solution.py
+++ b/solution.py
@@ -205,6 +205,7 @@
     stage_sem,
     grad_sem,
     ready,
+    inner_sides,
 ):
     def stage(source, target, sem):
         copy = pltpu.make_async_copy(source, target, sem)
@@ -352,9 +353,6 @@
                 for half in range(2):
                     exchange(CROSSING, half).start()
 
-    if remote:
-        pl.when(late == 1)(enter)
-
     staged_state.wait()
     staged_adjacency.wait()
     for v in range(5):
@@ -365,6 +363,8 @@
         staged_grad[b].wait()
         if b == REST_AFTER:
             staged_late = stage_rest()
+            if remote:
+                pl.when(late == 1)(enter)
         for k in range(K):
             near = jnp.broadcast_to(adjacency[k, :, b : b + 1], (5, CB))
             block = state[:, 0, :]
@@ -481,6 +481,14 @@
     lax.fori_loop(HOLD, TILES // 5, inner_tiles, 0)
 
     for side in range(2):
+        where = split_cells(inner_cells[pl.ds(side, 8, stride=2), :])
+        normal = normal_of(0)
+        out = rebuild(table, where, [-x for x in normal] if side else normal)
+        for v in range(5):
+            inner_sides[side, v] = out[v]
+
+
+    for side in range(2):
         if remote:
             receives = has_nxt if side else has_prv
 
@@ -506,8 +514,8 @@
     sweep = sweeps[0:8, :]
     left_cells = inner_cells[pl.ds(0, 8, stride=2), :]
     right_cells = inner_cells[pl.ds(1, 8, stride=2), :]
-    left = rebuild(table, split_cells(left_cells), normal)
-    right = rebuild(table, split_cells(right_cells), [-x for x in normal])
+    left = [inner_sides[0, v] for v in range(5)]
+    right = [inner_sides[1, v] for v in range(5)]
     flux = roe_flux(left, right, normal, sweep)
     scatter([-x for x in flux] + [sweep], left_cells, split.at[0], total)
     scatter(flux + [-sweep], right_cells, split.at[1], total)
@@ -606,6 +614,7 @@
             pltpu.SemaphoreType.DMA((7,)),
             pltpu.SemaphoreType.DMA((NB,)),
             pltpu.SemaphoreType.REGULAR((3,)),
+            pltpu.VMEM((2, 5, 8, CB), F32),
         ],
         compiler_params=pltpu.CompilerParams(**params),
     )(*inputs)

time: 20.8 us -> 20.6 us (level)
    pallas_call x1, Pallas kernels: 17.9 us -> 17.6 us  [section(): pl.pallas_call(functools.partial(kernel, remote), out_shape=jax.ShapeDtyp...]
where the time goes in v6:
time: 20.6 us; the launch traced here: 20.4 us
  Pallas kernels  19.1 us (93%)
  between operations  1.29 us (6%)
    pallas_call x1, Pallas kernels, section(): pl.pallas_call(functools.partial(kernel, remote), out_shape=jax.ShapeDtyp...  17.6 us
    pallas_call x1, Pallas kernels, section(): pl.pallas_call(finish, out_shape=(jax.ShapeDtypeStruct((5, NB, CB), F32),...  1.46 us

profile of v6, /device:TPU:199, one launch (start us, length us, event | category | flops | bytes accessed | tf_op | source)
XLA Modules:
  0.0 20.4 jit_solution(9409514972294743408)
XLA Ops:
  1.3 17.6 %shard_map.113.total = f32[64,128]{1,0:T(8,128)} custom-call(f32[5,4,128]{2,1,0:T(4,128)} %bitcast.25, bf16[4,3,128,384]{3,2,1,0:T(8,128)(2,1)} %bitcast.21, s32[3,1,4]{2,1,0:T(1,128)} %bitcast.30, f32[3,4,128]{2,1,0:T(4,128)} %bitcast.28, f32[3,200,128]{2,1,0:T(8,128)} %bitcast.23, s32[800,128]{1,0:T(8,128)} %bitcast.22, s32[16,128]{1,0:T(8,128)} %bitcast.27, ...), custom_call_target="tpu_custom_call" | custom-call | tf_op jit(solution)/shard_map/pallas_call | solution.py:596
  18.9 1.5 %shard_map.114 = (f32[5,4,128]{2,1,0:T(4,128)}, f32[4,128]{1,0:T(4,128)}) custom-call(f32[64,128]{1,0:T(8,128)} %shard_map.113.total, f32[5,4,128]{2,1,0:T(4,128)} %bitcast.26, f32[4,128]{1,0:T(4,128)} %bitcast.29, s32[1,1]{1,0:T(1,128)S(6)} %copy.18.counts), custom_call_target="tpu_custom_call" | custom-call | tf_op jit(solution)/shard_map/pallas_call | solution.py:621

commit v7 on v6

--- a/solution.py
+++ b/solution.py
@@ -167,7 +167,7 @@
             at = jnp.broadcast_to(lanes[i : i + 1, :], (CB, CB)).astype(BF16)
             right.append(jnp.where(at == slot, one, zero))
         left, right = jnp.concatenate(left, axis=1), jnp.concatenate(right, axis=1)
-        part = lax.dot_general(left, right, (((1,), (1,)), ((), ())), preferred_element_type=F32)
+        part = lax.dot_general(right, left, (((1,), (1,)), ((), ())), preferred_element_type=F32)
         result = part if result is None else result + part
     total[...] += result
 
@@ -578,9 +578,10 @@
 
 def finish(total, state, volume, counts, content, new_volume):
     live = jnp.broadcast_to(counts[...], (8, CB))
+    flat = total[...].T
     for h in range(4):
         on = live > h
-        sums = total[h * 16 : h * 16 + 6, :] + total[h * 16 + 6 : h * 16 + 12, :]
+        sums = flat[h * 16 : h * 16 + 6, :] + flat[h * 16 + 6 : h * 16 + 12, :]
         room = volume[h : h + 1, :]
         content[:, h, :] = room * state[:, h, :] + jnp.where(on[0:5], STEP_SIZE * sums[0:5, :], 0.0)
         new_volume[h : h + 1, :] = room + jnp.where(on[0:1], sums[5:6, :], 0.0)
@@ -595,7 +596,7 @@
     inputs = (state, grad, adjacency, node_vel, face_normal, face_nodes, inner_cells, iface_cells)
     total = pl.pallas_call(
         functools.partial(kernel, remote),
-        out_shape=jax.ShapeDtypeStruct((64, CB), F32),
+        out_shape=jax.ShapeDtypeStruct((CB, 64), F32),
         in_specs=[hbm] * 8,
         out_specs=vmem,
         scratch_shapes=[

time: 20.6 us -> 20.6 us (level)
  no operation moved by 1% of the time
where the time goes in v7:
time: 20.6 us; the launch traced here: 20.5 us
  Pallas kernels  19.2 us (93%)
  between operations  1.29 us (6%)
    pallas_call x1, Pallas kernels, section(): pl.pallas_call(functools.partial(kernel, remote), out_shape=jax.ShapeDtyp...  17.6 us
    pallas_call x1, Pallas kernels, section(): pl.pallas_call(finish, out_shape=(jax.ShapeDtypeStruct((5, NB, CB), F32),...  1.57 us

profile of v7, /device:TPU:199, one launch (start us, length us, event | category | flops | bytes accessed | tf_op | source)
XLA Modules:
  0.0 20.5 jit_solution(9529007169089317708)
XLA Ops:
  1.3 17.6 %shard_map.113.total = f32[128,64]{1,0:T(8,128)} custom-call(f32[5,4,128]{2,1,0:T(4,128)} %bitcast.25, bf16[4,3,128,384]{3,2,1,0:T(8,128)(2,1)} %bitcast.21, s32[3,1,4]{2,1,0:T(1,128)} %bitcast.30, f32[3,4,128]{2,1,0:T(4,128)} %bitcast.28, f32[3,200,128]{2,1,0:T(8,128)} %bitcast.23, s32[800,128]{1,0:T(8,128)} %bitcast.22, s32[16,128]{1,0:T(8,128)} %bitcast.27, ...), custom_call_target="tpu_custom_call" | custom-call | tf_op jit(solution)/shard_map/pallas_call | solution.py:597
  18.9 1.6 %shard_map.114 = (f32[5,4,128]{2,1,0:T(4,128)}, f32[4,128]{1,0:T(4,128)}) custom-call(f32[128,64]{1,0:T(8,128)} %shard_map.113.total, f32[5,4,128]{2,1,0:T(4,128)} %bitcast.26, f32[4,128]{1,0:T(4,128)} %bitcast.29, s32[1,1]{1,0:T(1,128)S(6)} %copy.18.counts), custom_call_target="tpu_custom_call" | custom-call | tf_op jit(solution)/shard_map/pallas_call | solution.py:622
